TPU v7x, 32 devices: a whole 2x2x4 slice. The times are simulated.
32 devices in a mesh: gr: 4 (over z), gc: 8 (over y, x, core).
Axes of the slice: x: 2, y: 2, z: 4, core: 2. Of those that a mesh axis runs over, the one named last changes fastest.
Arguments:
- student: bfloat16 [4096, 1024], P(('gr', 'gc')), may hold values from -500 to 500
- teacher: bfloat16 [4096, 1024], P(('gr', 'gc')), may hold values from -500 to 500
Outputs:
- student_grad: float32 [4096, 1024], P(('gr', 'gc'))
All inputs are finite; a program needn't handle non-finite values.
Results may differ from a plain program's by a relative error of at most 0.0085.
Values may be sent and summed in bfloat16 or wider, within the bound.
No kernel may reach another device: no remote copies, remote signals or barrier semaphores. Data moves between devices by JAX's collectives and lax.ppermute only.
A program may use at most 64 MiB of HBM per device.

v0:
```python
import functools

import jax
import jax.numpy as jnp
from jax import lax
from jax.experimental import pallas as pl
from jax.experimental.pallas import tpu as pltpu
from jax.sharding import PartitionSpec as P


F32, BF16 = jnp.float32, jnp.bfloat16
VM = pl.BlockSpec(memory_space=pltpu.VMEM)


def inverse_rms(values):
    return lax.rsqrt(jnp.mean(values * values, axis=-1, keepdims=True) + 1e-06)


def unit_of(rows):
    values = rows.astype(F32)
    return (values * inverse_rms(values) * rows.shape[-1] ** (-0.5)).astype(BF16)


def nt(a, b):
    return lax.dot_general(a, b, (((1,), (1,)), ((), ())), preferred_element_type=F32)


def tn(a, b):
    return lax.dot_general(a, b, (((0,), (0,)), ((), ())), preferred_element_type=F32)


def nn(a, b):
    return lax.dot_general(a, b, (((1,), (0,)), ((), ())), preferred_element_type=F32)


def call(kernel, outs, *args, flops=0, into=()):
    size = sum(a.size * a.dtype.itemsize for a in args)
    size += sum(o.size * o.dtype.itemsize for o in outs)
    return pl.pallas_call(
        kernel,
        out_shape=outs,
        in_specs=[VM] * len(args),
        out_specs=[VM] * len(outs),
        input_output_aliases={i: i for i in into},
        cost_estimate=pl.CostEstimate(flops=flops, bytes_accessed=size, transcendentals=0),
        compiler_params=pltpu.CompilerParams(vmem_limit_bytes=24 << 20),
    )(*args)


def shape(rows, cols, dtype):
    return jax.ShapeDtypeStruct((rows, cols), dtype)


def store_units(out, starts, raws):
    for at, raw in zip(starts, raws):
        out[pl.ds(at, raw.shape[0]), :] = unit_of(raw[...])


def pull_of(rows_s, rows_t, block_s, block_t):
    stretch = 0.5 * rows_s.shape[1] ** 0.5
    total = None
    half = block_s.shape[0] // 2
    for i in range(2):
        at = pl.ds(i * half, half)
        sim = nt(block_s[at, :], rows_s) - nt(block_t[at, :], rows_t)
        term = tn(jnp.tanh(stretch * sim).astype(BF16), block_s[at, :])
        total = term if total is None else total + term
    return total


def own_kernel(student, teacher, unit_s, unit_t, scale):
    values = student[...].astype(F32)
    inverse = inverse_rms(values)
    unit_s[...] = (values * inverse * values.shape[-1] ** (-0.5)).astype(BF16)
    unit_t[...] = unit_of(teacher[...])
    scale[...] = jnp.broadcast_to(inverse, scale.shape)


def early_kernel(starts, own_s, own_t, *refs):
    *raws, block_s, block_t = refs
    n = len(starts)
    block_s[pl.ds(0, own_s.shape[0]), :] = own_s[...]
    block_t[pl.ds(0, own_s.shape[0]), :] = own_t[...]
    store_units(block_s, starts, raws[:n])
    store_units(block_t, starts, raws[n:])


def lift_kernel(size, block_s, *refs):
    *raws, once_s, product = refs
    rows = raws[0].shape[0]
    store_units(once_s, range(0, len(raws) * rows, rows), raws)
    at = pl.ds(0, size)
    product[at, :] = nt(block_s[at, :], once_s[...])


def more_kernel(starts, block_s, block_t, product, once_s, *refs):
    *raws, out_s, out_t, out = refs
    n = len(starts)
    rows = raws[0].shape[0]
    units = jnp.concatenate([unit_of(r[...]) for r in raws[:n]], axis=0)
    part = nt(units, once_s[...])
    for i, start in enumerate(starts):
        out_s[pl.ds(start, rows), :] = units[i * rows : (i + 1) * rows]
        out[pl.ds(start, rows), :] = part[i * rows : (i + 1) * rows]
    store_units(out_t, starts, raws[n:])


def once_kernel(block_t, product, *refs):
    *raws, kept, sent = refs
    stretch = 0.5 * block_t.shape[1] ** 0.5
    once_t = jnp.concatenate([unit_of(r[...]) for r in raws], axis=0)
    half = kept.shape[0]
    for start, out in ((half, sent), (0, kept)):
        at = pl.ds(start, half)
        sim = product[at, :] - nt(block_t[at, :], once_t)
        out[...] = jnp.tanh(stretch * sim).astype(BF16)


def back_kernel(block_s, kept, sent, *back):
    half = kept.shape[0]
    sums = tn(kept[...], block_s[pl.ds(0, half), :]) + tn(sent[...], block_s[pl.ds(half, half), :])
    rows = back[0].shape[0]
    for i, out in enumerate(back):
        out[...] = sums[i * rows : (i + 1) * rows].astype(BF16)


def both_kernel(n_both, block_s, block_t, *refs):
    raw_s, raw_t, back = refs[:n_both], refs[n_both : 2 * n_both], refs[2 * n_both :]
    for i in range(n_both):
        rows_s, rows_t = unit_of(raw_s[i][...]), unit_of(raw_t[i][...])
        back[i][...] = pull_of(rows_s, rows_t, block_s, block_t).astype(BF16)


def near_kernel(own_s, own_t, block_s, block_t, pull):
    pull[...] = pull_of(own_s[...], own_t[...], block_s, block_t)


def pack_kernel(n_pack, kept, came, once_s, mate_s, *outs):
    rows, half = outs[-1].shape[0], kept.shape[1]
    for k, out in enumerate(outs):
        at = pl.ds(k * rows, rows)
        if k < n_pack:
            out[:, pl.ds(0, half)] = kept[at, :]
            out[:, pl.ds(half, half)] = came[at, :]
        else:
            out[...] = (nn(kept[at, :], once_s[...]) + nn(came[at, :], mate_s[...])).astype(BF16)


def met_kernel(n, before, *refs):
    weights, units, pull = refs[:n], refs[n:-1], refs[-1]
    total = before[...]
    for k, weight in enumerate(weights):
        block = jnp.concatenate([units[2 * k][...], units[2 * k + 1][...]], axis=0)
        total += nn(weight[...], block)
    pull[...] = total


def end_kernel(factor, own_s, scale, *refs):
    *terms, out = refs
    unit = own_s[...].astype(F32)
    pull = terms[0][...]
    for term in terms[1:]:
        pull = pull + term[...].astype(F32)
    radial = jnp.sum(unit * pull, axis=-1, keepdims=True)
    out[...] = factor * scale[:, :1] * (pull - radial * unit)


def local(n_gr, n_gc, student, teacher):
    rows, width = student.shape
    axes = ("gr", "gc")

    def shift(x, pairs):
        return lax.ppermute(x, axes, pairs)

    def across(x, mask):
        pairs = [(g * n_gc + c, g * n_gc + (c ^ mask)) for g in range(n_gr) for c in range(n_gc)]
        return shift(x, pairs)

    order = []
    for i in range(n_gr):
        order.append(i // 2 if i % 2 == 0 else n_gr - 1 - i // 2)

    def along(x, step):
        pairs = []
        for i in range(n_gr):
            a, b = order[i], order[(i + step) % n_gr]
            pairs += [(a * n_gc + c, b * n_gc + c) for c in range(n_gc)]
        return shift(x, pairs)

    def run(kernel, outs, *args, flops=0, into=()):
        return call(kernel, outs, *args, flops=flops, into=into)

    once = list(range(1, (n_gr + 1) // 2))
    both = [n_gr // 2] if n_gr % 2 == 0 else []
    n_once, n_both = len(once), len(both)
    once_rows = n_once * rows
    far_s = [along(student, d) for d in once + both]
    far_t = [along(teacher, d) for d in once + both]

    even = list(range(0, n_gc, 2))
    early = [k for k in even if k & (k - 1) == 0]
    late = [k for k in even if k not in early]
    mid = [k + 1 for k in early]
    last = late + [k + 1 for k in late]
    half = rows * len(even)
    work = 2 * rows * width

    got_s, got_t = {0: student}, {0: teacher}
    for k in even[1:]:
        high = 1 << (k.bit_length() - 1)
        low = k & -k
        got_s[k] = across(got_s[k ^ high], high)
        got_t[k] = across(got_t[k ^ low], low)
    for k in even:
        got_s[k + 1] = across(got_s[k], 1)
        got_t[k + 1] = across(got_t[k], 1)

    def raws(slots):
        return [got_s[k] for k in slots] + [got_t[k] for k in slots]

    order_of = early + late
    place = {k: i * rows for i, k in enumerate(order_of + [k + 1 for k in order_of])}

    def starts(slots):
        return [place[k] for k in slots]

    total = n_gc * rows
    pull_shape = shape(rows, width, F32)
    block_shape = shape(total, width, BF16)
    own_s, own_t, scale = run(
        own_kernel, [shape(rows, width, BF16)] * 2 + [shape(rows, 128, F32)], student, teacher
    )
    block_s, block_t = run(
        functools.partial(early_kernel, starts(early[1:])),
        [block_shape] * 2,
        own_s,
        own_t,
        *raws(early[1:]),
    )
    once_s, product = run(
        functools.partial(lift_kernel, len(early) * rows),
        [shape(once_rows, width, BF16), shape(total, once_rows, F32)],
        block_s,
        *far_s[:n_once],
        flops=len(early) * once_rows * work,
    )
    mates = {k: across(once_s, k) for k in early[1:]}
    mates[0] = once_s
    for k in early:
        mates[k + 1] = across(mates[k], 1)

    for slots in (mid, last):
        block_s, block_t, product = run(
            functools.partial(more_kernel, starts(slots)),
            [block_shape, block_shape, shape(total, once_rows, F32)],
            block_s,
            block_t,
            product,
            once_s,
            *raws(slots),
            flops=len(slots) * once_rows * work,
            into=(0, 1, 2),
        )
    kept, sent = run(
        once_kernel,
        [shape(half, once_rows, BF16)] * 2,
        block_t,
        product,
        *far_t[:n_once],
        flops=n_gc * once_rows * work,
    )
    came = across(sent, 1)
    back = run(
        back_kernel,
        [shape(rows, width, BF16)] * n_once,
        block_s,
        kept,
        sent,
        flops=n_gc * once_rows * work,
    )
    home = [along(b, n_gr - d) for b, d in zip(back, once)]
    n_pack = len(early)
    packed = run(
        functools.partial(pack_kernel, n_pack),
        [shape(rows, 2 * once_rows, BF16)] * n_pack + [shape(rows, width, BF16)] * len(late),
        kept,
        came,
        once_s,
        mates[1],
        flops=len(late) * 2 * once_rows * work,
    )
    weights = [packed[0]] + [across(p, k) for p, k in zip(packed[1:], early[1:])]
    home += [across(p, k) for p, k in zip(packed[n_pack:], late)]
    back = run(
        functools.partial(both_kernel, n_both),
        [shape(rows, width, BF16)] * n_both,
        block_s,
        block_t,
        *far_s[n_once:],
        *far_t[n_once:],
        flops=3 * n_both * n_gc * rows * work,
    )
    home += [along(b, n_gr - d) for b, d in zip(back, both)]
    (pull,) = run(
        near_kernel, [pull_shape], own_s, own_t, block_s, block_t, flops=3 * n_gc * rows * work
    )
    (pull,) = run(
        functools.partial(met_kernel, n_pack),
        [pull_shape],
        pull,
        *weights,
        *[mates[k + c] for k in early for c in (0, 1)],
        flops=n_gc * once_rows * work,
    )
    factor = 12.0 * (width / (rows * n_gr * n_gc)) ** 0.5
    return run(functools.partial(end_kernel, factor), [pull_shape], own_s, scale, pull, *home)[0]


def solution(mesh):
    n_gr, n_gc = mesh.shape["gr"], mesh.shape["gc"]
    spec = P(("gr", "gc"), None)

    def body(student, teacher):
        return local(n_gr, n_gc, student, teacher)

    return jax.shard_map(
        body, mesh=mesh, in_specs=(spec, spec), out_specs=spec, check_vma=False
    )
```

profile of v0, /device:TPU:0, one launch (start us, length us, event | category | flops | bytes accessed | tf_op | source)
XLA Modules:
  0.0 65.2 jit_solution(7670260969711247606)
XLA Ops:
  0.0 3.0 %collective-permute-start = (bf16[128,1024]{1,0:T(8,128)(2,1)}, bf16[128,1024]{1,0:T(8,128)(2,1)S(1)}, u32[]{:S(2)}, u32[]{:S(2)}) collective-permute-start(bf16[128,1024]{1,0:T(8,128)(2,1)} %student.1), channel_id=1, source_target_pairs={{0,2},{1,3},{2,0},{3,1},{4,6},{5,7},{6,4},{7,5},{8,10},{9,11},{10,... | collective-permute-start | bytes 786440 | tf_op jit(solution)/shard_map/ppermute | solution.py:173
  3.0 1.5 %collective-permute-start.1 = (bf16[128,1024]{1,0:T(8,128)(2,1)}, bf16[128,1024]{1,0:T(8,128)(2,1)S(1)}, u32[]{:S(2)}, u32[]{:S(2)}) collective-permute-start(bf16[128,1024]{1,0:T(8,128)(2,1)} %student.1), channel_id=1, source_target_pairs={{0,4},{1,5},{2,6},{3,7},{4,0},{5,1},{6,2},{7,3},{8,12},{9,13},{10,... | collective-permute-start | bytes 786440 | tf_op jit(solution)/shard_map/ppermute | solution.py:173
  5.0 4.1 %collective-permute-start.4 = (bf16[128,1024]{1,0:T(8,128)(2,1)}, bf16[128,1024]{1,0:T(8,128)(2,1)S(1)}, u32[]{:S(2)}, u32[]{:S(2)}) collective-permute-start(bf16[128,1024]{1,0:T(8,128)(2,1)} %student.1), channel_id=1, source_target_pairs={{0,24},{1,25},{2,26},{3,27},{4,28},{5,29},{6,30},{7,31},{24,8},{25... | collective-permute-start | bytes 786440 | tf_op jit(solution)/shard_map/ppermute | solution.py:173
  9.1 1.2 %collective-permute-done.refs_0_ = bf16[128,1024]{1,0:T(8,128)(2,1)S(1)} collective-permute-done((bf16[128,1024]{1,0:T(8,128)(2,1)}, bf16[128,1024]{1,0:T(8,128)(2,1)S(1)}, u32[]{:S(2)}, u32[]{:S(2)}) %collective-permute-start) | collective-permute-done | bytes 262176 | tf_op jit(solution)/shard_map/ppermute | solution.py:173
  10.3 2.0 %collective-permute-done.1.refs_1_ = bf16[128,1024]{1,0:T(8,128)(2,1)S(1)} collective-permute-done((bf16[128,1024]{1,0:T(8,128)(2,1)}, bf16[128,1024]{1,0:T(8,128)(2,1)S(1)}, u32[]{:S(2)}, u32[]{:S(2)}) %collective-permute-start.1) | collective-permute-done | bytes 262176 | tf_op jit(solution)/shard_map/ppermute | solution.py:173
  12.4 2.7 %collective-permute-done.2.refs_2_ = bf16[128,1024]{1,0:T(8,128)(2,1)S(1)} collective-permute-done((bf16[128,1024]{1,0:T(8,128)(2,1)}, bf16[128,1024]{1,0:T(8,128)(2,1)S(1)}, u32[]{:S(2)}, u32[]{:S(2)}) %collective-permute-start.2) | collective-permute-done | bytes 262176 | tf_op jit(solution)/shard_map/ppermute | solution.py:173
  15.1 3.9 %collective-permute-start.15 = (bf16[128,1024]{1,0:T(8,128)(2,1)}, bf16[128,1024]{1,0:T(8,128)(2,1)S(1)}, u32[]{:S(2)}, u32[]{:S(2)}) collective-permute-start(bf16[128,1024]{1,0:T(8,128)(2,1)} %teacher.1), channel_id=1, source_target_pairs={{0,24},{1,25},{2,26},{3,27},{4,28},{5,29},{6,30},{7,31},{24,8},{25... | collective-permute-start | bytes 786440 | tf_op jit(solution)/shard_map/ppermute | solution.py:173
  19.0 6.9 %collective-permute-done.4.refs_0_ = bf16[128,1024]{1,0:T(8,128)(2,1)S(1)} collective-permute-done((bf16[128,1024]{1,0:T(8,128)(2,1)}, bf16[128,1024]{1,0:T(8,128)(2,1)S(1)}, u32[]{:S(2)}, u32[]{:S(2)}) %collective-permute-start.4) | collective-permute-done | bytes 262176 | tf_op jit(solution)/shard_map/ppermute | solution.py:173
  25.8 1.6 %collective-permute-start.11 = (bf16[128,1024]{1,0:T(8,128)(2,1)S(1)}, bf16[128,1024]{1,0:T(8,128)(2,1)S(1)}, u32[]{:S(2)}, u32[]{:S(2)}) collective-permute-start(bf16[128,1024]{1,0:T(8,128)(2,1)S(1)} %collective-permute-done.refs_0_), channel_id=1, source_target_pairs={{0,4},{1,5},{2,6},{3,7},{4,0},{5,1},{6,2},{7,3},{8,12},{9,13},{10,... | collective-permute-start | bytes 786440 | tf_op jit(solution)/shard_map/ppermute | solution.py:173
  27.4 1.5 %collective-permute-start.13 = (bf16[128,1024]{1,0:T(8,128)(2,1)S(1)}, bf16[128,1024]{1,0:T(8,128)(2,1)S(1)}, u32[]{:S(2)}, u32[]{:S(2)}) collective-permute-start(bf16[128,1024]{1,0:T(8,128)(2,1)S(1)} %collective-permute-done.3.refs_3_), channel_id=1, source_target_pairs={{0,2},{1,3},{2,0},{3,1},{4,6},{5,7},{6,4},{7,5},{8,10},{9,11},{10,... | collective-permute-start | bytes 786440 | tf_op jit(solution)/shard_map/ppermute | solution.py:173
  28.9 1.4 %collective-permute-done.15.refs_0_ = bf16[128,1024]{1,0:T(8,128)(2,1)S(1)} collective-permute-done((bf16[128,1024]{1,0:T(8,128)(2,1)}, bf16[128,1024]{1,0:T(8,128)(2,1)S(1)}, u32[]{:S(2)}, u32[]{:S(2)}) %collective-permute-start.15) | collective-permute-done | bytes 262176 | tf_op jit(solution)/shard_map/ppermute | solution.py:173
  30.9 1.3 %collective-permute-done.11.refs_0_ = bf16[128,1024]{1,0:T(8,128)(2,1)S(1)} collective-permute-done((bf16[128,1024]{1,0:T(8,128)(2,1)S(1)}, bf16[128,1024]{1,0:T(8,128)(2,1)S(1)}, u32[]{:S(2)}, u32[]{:S(2)}) %collective-permute-start.11) | collective-permute-done | bytes 262176 | tf_op jit(solution)/shard_map/ppermute | solution.py:173
  32.2 1.6 %collective-permute-done.13.refs_2_ = bf16[128,1024]{1,0:T(8,128)(2,1)S(1)} collective-permute-done((bf16[128,1024]{1,0:T(8,128)(2,1)S(1)}, bf16[128,1024]{1,0:T(8,128)(2,1)S(1)}, u32[]{:S(2)}, u32[]{:S(2)}) %collective-permute-start.13) | collective-permute-done | bytes 262176 | tf_op jit(solution)/shard_map/ppermute | solution.py:173
  33.8 1.0 %copy-done = bf16[128,1024]{1,0:T(8,128)(2,1)S(1)} copy-done((bf16[128,1024]{1,0:T(8,128)(2,1)S(1)}, bf16[128,1024]{1,0:T(8,128)(2,1)}, u32[]{:S(2)}) %copy-start) | copy-done | bytes 262168
  34.8 0.9 %copy-done.1 = bf16[128,1024]{1,0:T(8,128)(2,1)S(1)} copy-done((bf16[128,1024]{1,0:T(8,128)(2,1)S(1)}, bf16[128,1024]{1,0:T(8,128)(2,1)}, u32[]{:S(2)}) %copy-start.1) | copy-done | bytes 262168
  36.9 1.6 %collective-permute-start.20 = (bf16[128,1024]{1,0:T(8,128)(2,1)S(1)}, bf16[128,1024]{1,0:T(8,128)(2,1)S(1)}, u32[]{:S(2)}, u32[]{:S(2)}) collective-permute-start(bf16[128,1024]{1,0:T(8,128)(2,1)S(1)} %get-tuple-element.30.once_s.refs_3_), channel_id=1, source_target_pairs={{0,2},{1,3},{2,0},{3,1},{4,6},{5,7},{6,4},{7,5},{8,10},{9,11},{10,... | collective-permute-start | bytes 786440 | tf_op jit(solution)/shard_map/ppermute | solution.py:173
  38.9 2.0 %collective-permute-start.27 = (bf16[128,1024]{1,0:T(8,128)(2,1)S(1)}, bf16[128,1024]{1,0:T(8,128)(2,1)S(1)}, u32[]{:S(2)}, u32[]{:S(2)}) collective-permute-start(bf16[128,1024]{1,0:T(8,128)(2,1)S(1)} %copy-done.1), channel_id=1, source_target_pairs={{0,8},{1,9},{2,10},{3,11},{4,12},{5,13},{6,14},{7,15},{24,16},{25,... | collective-permute-start | bytes 786440 | tf_op jit(solution)/shard_map/ppermute | solution.py:173
  41.0 0.7 %shard_map.31 = (bf16[1024,1024]{1,0:T(8,128)(2,1)S(1)}, bf16[1024,1024]{1,0:T(8,128)(2,1)S(1)}, f32[1024,128]{1,0:T(8,128)S(1)}) custom-call(bf16[1024,1024]{1,0:T(8,128)(2,1)S(1)} %get-tuple-element.27.block_s, bf16[1024,1024]{1,0:T(8,128)(2,1)S(1)} %get-tuple-element.28.block_t, ...), custom_call_target="tpu_custom_call", output_to_operand_aliasing={{0}: (0, {}), {1}: (1, {}), {2}: (2, {})} | custom-call | flops 100663296 | bytes 11272192 | tf_op jit(solution)/shard_map/pallas_call | solution.py:39
  42.1 0.8 %shard_map.34 = (bf16[512,128]{1,0:T(8,128)(2,1)S(1)}, bf16[512,128]{1,0:T(8,128)(2,1)S(1)}) custom-call(bf16[1024,1024]{1,0:T(8,128)(2,1)S(1)} %get-tuple-element.35.block_t, f32[1024,128]{1,0:T(8,128)S(1)} %get-tuple-element.36.product, bf16[128,1024]{1,0:T(8,128)(2,1)S(1)} %collective-permute-done.15.refs_0_), custom_call_target="tpu_custom_call" | custom-call | flops 268435456 | bytes 3145728 | tf_op jit(solution)/shard_map/pallas_call | solution.py:39
  43.6 2.1 %collective-permute-done.20.refs_5_ = bf16[128,1024]{1,0:T(8,128)(2,1)S(1)} collective-permute-done((bf16[128,1024]{1,0:T(8,128)(2,1)S(1)}, bf16[128,1024]{1,0:T(8,128)(2,1)S(1)}, u32[]{:S(2)}, u32[]{:S(2)}) %collective-permute-start.20) | collective-permute-done | bytes 262176 | tf_op jit(solution)/shard_map/ppermute | solution.py:173
  45.7 1.2 %collective-permute-done.22.refs_7_ = bf16[128,1024]{1,0:T(8,128)(2,1)S(1)} collective-permute-done((bf16[128,1024]{1,0:T(8,128)(2,1)S(1)}, bf16[128,1024]{1,0:T(8,128)(2,1)S(1)}, u32[]{:S(2)}, u32[]{:S(2)}) %collective-permute-start.22) | collective-permute-done | bytes 262176 | tf_op jit(solution)/shard_map/ppermute | solution.py:173
  47.4 1.0 %collective-permute-done.27.refs_1_ = bf16[128,1024]{1,0:T(8,128)(2,1)S(1)} collective-permute-done((bf16[128,1024]{1,0:T(8,128)(2,1)S(1)}, bf16[128,1024]{1,0:T(8,128)(2,1)S(1)}, u32[]{:S(2)}, u32[]{:S(2)}) %collective-permute-start.27) | collective-permute-done | bytes 262176 | tf_op jit(solution)/shard_map/ppermute | solution.py:173
  48.4 1.7 %collective-permute-start.24 = (bf16[128,1024]{1,0:T(8,128)(2,1)S(1)}, bf16[128,1024]{1,0:T(8,128)(2,1)S(1)}, u32[]{:S(2)}, u32[]{:S(2)}) collective-permute-start(bf16[128,1024]{1,0:T(8,128)(2,1)S(1)} %shard_map.37), channel_id=1, source_target_pairs={{0,16},{1,17},{2,18},{3,19},{4,20},{5,21},{6,22},{7,23},{24,0},{25... | collective-permute-start | bytes 786440 | tf_op jit(solution)/shard_map/ppermute | solution.py:173
  50.1 1.9 %shard_map.38 = bf16[128,1024]{1,0:T(8,128)(2,1)S(1)} custom-call(bf16[1024,1024]{1,0:T(8,128)(2,1)S(1)} %get-tuple-element.34.block_s, bf16[1024,1024]{1,0:T(8,128)(2,1)S(1)} %get-tuple-element.35.block_t, bf16[128,1024]{1,0:T(8,128)(2,1)S(1)} %collective-permute-done.26.refs_0_, bf16[128,1024]{1,0:T(8,128)(2,1)S(1)} %collective-permute-done.27.refs_1_), custom_call_target="tpu_custom_call" | custom-call | flops 805306368 | bytes 4980736 | tf_op jit(solution)/shard_map/pallas_call | solution.py:39
  52.0 0.9 %collective-permute-start.28 = (bf16[128,1024]{1,0:T(8,128)(2,1)S(1)}, bf16[128,1024]{1,0:T(8,128)(2,1)S(1)}, u32[]{:S(2)}, u32[]{:S(2)}) collective-permute-start(bf16[128,1024]{1,0:T(8,128)(2,1)S(1)} %shard_map.38), channel_id=1, source_target_pairs={{0,8},{1,9},{2,10},{3,11},{4,12},{5,13},{6,14},{7,15},{24,16},{25,... | collective-permute-start | bytes 786440 | tf_op jit(solution)/shard_map/ppermute | solution.py:173
  53.1 1.2 %collective-permute-start.25 = (bf16[128,1024]{1,0:T(8,128)(2,1)S(1)}, bf16[128,1024]{1,0:T(8,128)(2,1)S(1)}, u32[]{:S(2)}, u32[]{:S(2)}) collective-permute-start(bf16[128,1024]{1,0:T(8,128)(2,1)S(1)} %get-tuple-element.42), channel_id=1, source_target_pairs={{0,6},{1,7},{2,4},{3,5},{4,2},{5,3},{6,0},{7,1},{8,14},{9,15},{10,... | collective-permute-start | bytes 786440 | tf_op jit(solution)/shard_map/ppermute | solution.py:173
  54.4 1.5 %collective-permute-start.18 = (bf16[128,256]{1,0:T(8,128)(2,1)S(1)}, bf16[128,256]{1,0:T(8,128)(2,1)S(1)}, u32[]{:S(2)}, u32[]{:S(2)}) collective-permute-start(bf16[128,256]{1,0:T(8,128)(2,1)S(1)} %get-tuple-element.40), channel_id=1, source_target_pairs={{0,2},{1,3},{2,0},{3,1},{4,6},{5,7},{6,4},{7,5},{8,10},{9,11},{10,... | collective-permute-start | bytes 196616 | tf_op jit(solution)/shard_map/ppermute | solution.py:173
  55.9 0.8 %collective-permute-start.19 = (bf16[128,256]{1,0:T(8,128)(2,1)S(1)}, bf16[128,256]{1,0:T(8,128)(2,1)S(1)}, u32[]{:S(2)}, u32[]{:S(2)}) collective-permute-start(bf16[128,256]{1,0:T(8,128)(2,1)S(1)} %get-tuple-element.41), channel_id=1, source_target_pairs={{0,4},{1,5},{2,6},{3,7},{4,0},{5,1},{6,2},{7,3},{8,12},{9,13},{10,... | collective-permute-start | bytes 196616 | tf_op jit(solution)/shard_map/ppermute | solution.py:173
  56.7 1.7 %shard_map.33.before = f32[128,1024]{1,0:T(8,128)S(1)} custom-call(bf16[128,1024]{1,0:T(8,128)(2,1)S(1)} %get-tuple-element.24.own_s, bf16[128,1024]{1,0:T(8,128)(2,1)S(1)} %get-tuple-element.26.own_t, bf16[1024,1024]{1,0:T(8,128)(2,1)S(1)} %get-tuple-element.34.block_s, bf16[1024,1024]{1,0:T(8,128)(2,1)S(1)} %get-tuple-element.35.block_t), custom_call_target="tpu_custom_call" | custom-call | flops 805306368 | bytes 5242880 | tf_op jit(solution)/shard_map/pallas_call | solution.py:39
  58.4 4.4 %collective-permute-done.18.refs_1_ = bf16[128,256]{1,0:T(8,128)(2,1)S(1)} collective-permute-done((bf16[128,256]{1,0:T(8,128)(2,1)S(1)}, bf16[128,256]{1,0:T(8,128)(2,1)S(1)}, u32[]{:S(2)}, u32[]{:S(2)}) %collective-permute-start.18) | collective-permute-done | bytes 65568 | tf_op jit(solution)/shard_map/ppermute | solution.py:173
  62.7 0.9 %collective-permute-done.19.refs_2_ = bf16[128,256]{1,0:T(8,128)(2,1)S(1)} collective-permute-done((bf16[128,256]{1,0:T(8,128)(2,1)S(1)}, bf16[128,256]{1,0:T(8,128)(2,1)S(1)}, u32[]{:S(2)}, u32[]{:S(2)}) %collective-permute-start.19) | collective-permute-done | bytes 65568 | tf_op jit(solution)/shard_map/ppermute | solution.py:173
  64.1 1.1 %shard_map.39 = f32[128,1024]{1,0:T(8,128)} custom-call(bf16[128,1024]{1,0:T(8,128)(2,1)S(1)} %get-tuple-element.24.own_s, f32[128,128]{1,0:T(8,128)S(1)} %get-tuple-element.25.scale, f32[128,1024]{1,0:T(8,128)S(1)} %shard_map.36.refs_0_, bf16[128,1024]{1,0:T(8,128)(2,1)S(1)} %collective-permute-done.24.refs_1_, ...), custom_call_target="tpu_custom_call" | custom-call | bytes 2162688 | tf_op jit(solution)/shard_map/pallas_call | solution.py:39
  (42 shorter events, 4.9 us)
Async XLA Ops:
  0.0 10.3 %collective-permute-start = (bf16[128,1024]{1,0:T(8,128)(2,1)}, bf16[128,1024]{1,0:T(8,128)(2,1)S(1)}, u32[]{:S(2)}, u32[]{:S(2)}) collective-permute-start(bf16[128,1024]{1,0:T(8,128)(2,1)} %student.1), channel_id=1, source_target_pairs={{0,2},{1,3},{2,0},{3,1},{4,6},{5,7},{6,4},{7,5},{8,10},{9,11},{10,... | collective-permute-start | bytes 786440 | tf_op jit(solution)/shard_map/ppermute | solution.py:173
  3.0 9.4 %collective-permute-start.1 = (bf16[128,1024]{1,0:T(8,128)(2,1)}, bf16[128,1024]{1,0:T(8,128)(2,1)S(1)}, u32[]{:S(2)}, u32[]{:S(2)}) collective-permute-start(bf16[128,1024]{1,0:T(8,128)(2,1)} %student.1), channel_id=1, source_target_pairs={{0,4},{1,5},{2,6},{3,7},{4,0},{5,1},{6,2},{7,3},{8,12},{9,13},{10,... | collective-permute-start | bytes 786440 | tf_op jit(solution)/shard_map/ppermute | solution.py:173
  4.5 10.6 %collective-permute-start.2 = (bf16[128,1024]{1,0:T(8,128)(2,1)}, bf16[128,1024]{1,0:T(8,128)(2,1)S(1)}, u32[]{:S(2)}, u32[]{:S(2)}) collective-permute-start(bf16[128,1024]{1,0:T(8,128)(2,1)} %teacher.1), channel_id=1, source_target_pairs={{0,2},{1,3},{2,0},{3,1},{4,6},{5,7},{6,4},{7,5},{8,10},{9,11},{10,... | collective-permute-start | bytes 786440 | tf_op jit(solution)/shard_map/ppermute | solution.py:173
  5.0 13.9 %collective-permute-start.3 = (bf16[128,1024]{1,0:T(8,128)(2,1)}, bf16[128,1024]{1,0:T(8,128)(2,1)S(1)}, u32[]{:S(2)}, u32[]{:S(2)}) collective-permute-start(bf16[128,1024]{1,0:T(8,128)(2,1)} %teacher.1), channel_id=1, source_target_pairs={{0,4},{1,5},{2,6},{3,7},{4,0},{5,1},{6,2},{7,3},{8,12},{9,13},{10,... | collective-permute-start | bytes 786440 | tf_op jit(solution)/shard_map/ppermute | solution.py:173
  5.0 20.8 %collective-permute-start.4 = (bf16[128,1024]{1,0:T(8,128)(2,1)}, bf16[128,1024]{1,0:T(8,128)(2,1)S(1)}, u32[]{:S(2)}, u32[]{:S(2)}) collective-permute-start(bf16[128,1024]{1,0:T(8,128)(2,1)} %student.1), channel_id=1, source_target_pairs={{0,24},{1,25},{2,26},{3,27},{4,28},{5,29},{6,30},{7,31},{24,8},{25... | collective-permute-start | bytes 786440 | tf_op jit(solution)/shard_map/ppermute | solution.py:173
  10.3 17.1 %collective-permute-start.5 = (bf16[128,1024]{1,0:T(8,128)(2,1)}, bf16[128,1024]{1,0:T(8,128)(2,1)S(1)}, u32[]{:S(2)}, u32[]{:S(2)}) collective-permute-start(bf16[128,1024]{1,0:T(8,128)(2,1)} %student.1), channel_id=1, source_target_pairs={{0,1},{1,0},{2,3},{3,2},{4,5},{5,4},{6,7},{7,6},{8,9},{9,8},{10,11... | collective-permute-start | bytes 786440 | tf_op jit(solution)/shard_map/ppermute | solution.py:173
  12.4 16.6 %collective-permute-start.8 = (bf16[128,1024]{1,0:T(8,128)(2,1)}, bf16[128,1024]{1,0:T(8,128)(2,1)S(1)}, u32[]{:S(2)}, u32[]{:S(2)}) collective-permute-start(bf16[128,1024]{1,0:T(8,128)(2,1)} %teacher.1), channel_id=1, source_target_pairs={{0,1},{1,0},{2,3},{3,2},{4,5},{5,4},{6,7},{7,6},{8,9},{9,8},{10,11... | collective-permute-start | bytes 786440 | tf_op jit(solution)/shard_map/ppermute | solution.py:173
  15.1 15.3 %collective-permute-start.15 = (bf16[128,1024]{1,0:T(8,128)(2,1)}, bf16[128,1024]{1,0:T(8,128)(2,1)S(1)}, u32[]{:S(2)}, u32[]{:S(2)}) collective-permute-start(bf16[128,1024]{1,0:T(8,128)(2,1)} %teacher.1), channel_id=1, source_target_pairs={{0,24},{1,25},{2,26},{3,27},{4,28},{5,29},{6,30},{7,31},{24,8},{25... | collective-permute-start | bytes 786440 | tf_op jit(solution)/shard_map/ppermute | solution.py:173
  19.0 11.4 %collective-permute-start.6 = (bf16[128,1024]{1,0:T(8,128)(2,1)S(1)}, bf16[128,1024]{1,0:T(8,128)(2,1)S(1)}, u32[]{:S(2)}, u32[]{:S(2)}) collective-permute-start(bf16[128,1024]{1,0:T(8,128)(2,1)S(1)} %collective-permute-done.refs_0_), channel_id=1, source_target_pairs={{0,1},{1,0},{2,3},{3,2},{4,5},{5,4},{6,7},{7,6},{8,9},{9,8},{10,11... | collective-permute-start | bytes 786440 | tf_op jit(solution)/shard_map/ppermute | solution.py:173
  25.8 6.4 %collective-permute-start.11 = (bf16[128,1024]{1,0:T(8,128)(2,1)S(1)}, bf16[128,1024]{1,0:T(8,128)(2,1)S(1)}, u32[]{:S(2)}, u32[]{:S(2)}) collective-permute-start(bf16[128,1024]{1,0:T(8,128)(2,1)S(1)} %collective-permute-done.refs_0_), channel_id=1, source_target_pairs={{0,4},{1,5},{2,6},{3,7},{4,0},{5,1},{6,2},{7,3},{8,12},{9,13},{10,... | collective-permute-start | bytes 786440 | tf_op jit(solution)/shard_map/ppermute | solution.py:173
  27.4 6.4 %collective-permute-start.13 = (bf16[128,1024]{1,0:T(8,128)(2,1)S(1)}, bf16[128,1024]{1,0:T(8,128)(2,1)S(1)}, u32[]{:S(2)}, u32[]{:S(2)}) collective-permute-start(bf16[128,1024]{1,0:T(8,128)(2,1)S(1)} %collective-permute-done.3.refs_3_), channel_id=1, source_target_pairs={{0,2},{1,3},{2,0},{3,1},{4,6},{5,7},{6,4},{7,5},{8,10},{9,11},{10,... | collective-permute-start | bytes 786440 | tf_op jit(solution)/shard_map/ppermute | solution.py:173
  28.9 4.9 %collective-permute-start.7 = (bf16[128,1024]{1,0:T(8,128)(2,1)S(1)}, bf16[128,1024]{1,0:T(8,128)(2,1)S(1)}, u32[]{:S(2)}, u32[]{:S(2)}) collective-permute-start(bf16[128,1024]{1,0:T(8,128)(2,1)S(1)} %collective-permute-done.1.refs_1_), channel_id=1, source_target_pairs={{0,1},{1,0},{2,3},{3,2},{4,5},{5,4},{6,7},{7,6},{8,9},{9,8},{10,11... | collective-permute-start | bytes 786440 | tf_op jit(solution)/shard_map/ppermute | solution.py:173
  30.4 6.5 %collective-permute-start.9 = (bf16[128,1024]{1,0:T(8,128)(2,1)S(1)}, bf16[128,1024]{1,0:T(8,128)(2,1)S(1)}, u32[]{:S(2)}, u32[]{:S(2)}) collective-permute-start(bf16[128,1024]{1,0:T(8,128)(2,1)S(1)} %collective-permute-done.2.refs_2_), channel_id=1, source_target_pairs={{0,1},{1,0},{2,3},{3,2},{4,5},{5,4},{6,7},{7,6},{8,9},{9,8},{10,11... | collective-permute-start | bytes 786440 | tf_op jit(solution)/shard_map/ppermute | solution.py:173
  30.4 8.1 %collective-permute-start.10 = (bf16[128,1024]{1,0:T(8,128)(2,1)S(1)}, bf16[128,1024]{1,0:T(8,128)(2,1)S(1)}, u32[]{:S(2)}, u32[]{:S(2)}) collective-permute-start(bf16[128,1024]{1,0:T(8,128)(2,1)S(1)} %collective-permute-done.3.refs_3_), channel_id=1, source_target_pairs={{0,1},{1,0},{2,3},{3,2},{4,5},{5,4},{6,7},{7,6},{8,9},{9,8},{10,11... | collective-permute-start | bytes 786440 | tf_op jit(solution)/shard_map/ppermute | solution.py:173
  32.2 6.8 %collective-permute-start.12 = (bf16[128,1024]{1,0:T(8,128)(2,1)S(1)}, bf16[128,1024]{1,0:T(8,128)(2,1)S(1)}, u32[]{:S(2)}, u32[]{:S(2)}) collective-permute-start(bf16[128,1024]{1,0:T(8,128)(2,1)S(1)} %collective-permute-done.11.refs_0_), channel_id=1, source_target_pairs={{0,1},{1,0},{2,3},{3,2},{4,5},{5,4},{6,7},{7,6},{8,9},{9,8},{10,11... | collective-permute-start | bytes 786440 | tf_op jit(solution)/shard_map/ppermute | solution.py:173
  33.8 7.2 %collective-permute-start.14 = (bf16[128,1024]{1,0:T(8,128)(2,1)S(1)}, bf16[128,1024]{1,0:T(8,128)(2,1)S(1)}, u32[]{:S(2)}, u32[]{:S(2)}) collective-permute-start(bf16[128,1024]{1,0:T(8,128)(2,1)S(1)} %collective-permute-done.13.refs_2_), channel_id=1, source_target_pairs={{0,1},{1,0},{2,3},{3,2},{4,5},{5,4},{6,7},{7,6},{8,9},{9,8},{10,11... | collective-permute-start | bytes 786440 | tf_op jit(solution)/shard_map/ppermute | solution.py:173
  33.8 9.4 %collective-permute-start.26 = (bf16[128,1024]{1,0:T(8,128)(2,1)}, bf16[128,1024]{1,0:T(8,128)(2,1)S(1)}, u32[]{:S(2)}, u32[]{:S(2)}) collective-permute-start(bf16[128,1024]{1,0:T(8,128)(2,1)} %student.1), channel_id=1, source_target_pairs={{0,8},{1,9},{2,10},{3,11},{4,12},{5,13},{6,14},{7,15},{24,16},{25,... | collective-permute-start | bytes 786440 | tf_op jit(solution)/shard_map/ppermute | solution.py:173
  33.8 1.0 %copy-start = (bf16[128,1024]{1,0:T(8,128)(2,1)S(1)}, bf16[128,1024]{1,0:T(8,128)(2,1)}, u32[]{:S(2)}) copy-start(bf16[128,1024]{1,0:T(8,128)(2,1)} %student.1) | copy-start | bytes 786436
  34.8 0.9 %copy-start.1 = (bf16[128,1024]{1,0:T(8,128)(2,1)S(1)}, bf16[128,1024]{1,0:T(8,128)(2,1)}, u32[]{:S(2)}) copy-start(bf16[128,1024]{1,0:T(8,128)(2,1)} %teacher.1) | copy-start | bytes 786436
  36.9 8.8 %collective-permute-start.20 = (bf16[128,1024]{1,0:T(8,128)(2,1)S(1)}, bf16[128,1024]{1,0:T(8,128)(2,1)S(1)}, u32[]{:S(2)}, u32[]{:S(2)}) collective-permute-start(bf16[128,1024]{1,0:T(8,128)(2,1)S(1)} %get-tuple-element.30.once_s.refs_3_), channel_id=1, source_target_pairs={{0,2},{1,3},{2,0},{3,1},{4,6},{5,7},{6,4},{7,5},{8,10},{9,11},{10,... | collective-permute-start | bytes 786440 | tf_op jit(solution)/shard_map/ppermute | solution.py:173
  38.4 8.4 %collective-permute-start.22 = (bf16[128,1024]{1,0:T(8,128)(2,1)S(1)}, bf16[128,1024]{1,0:T(8,128)(2,1)S(1)}, u32[]{:S(2)}, u32[]{:S(2)}) collective-permute-start(bf16[128,1024]{1,0:T(8,128)(2,1)S(1)} %get-tuple-element.30.once_s.refs_3_), channel_id=1, source_target_pairs={{0,4},{1,5},{2,6},{3,7},{4,0},{5,1},{6,2},{7,3},{8,12},{9,13},{10,... | collective-permute-start | bytes 786440 | tf_op jit(solution)/shard_map/ppermute | solution.py:173
  38.9 9.4 %collective-permute-start.27 = (bf16[128,1024]{1,0:T(8,128)(2,1)S(1)}, bf16[128,1024]{1,0:T(8,128)(2,1)S(1)}, u32[]{:S(2)}, u32[]{:S(2)}) collective-permute-start(bf16[128,1024]{1,0:T(8,128)(2,1)S(1)} %copy-done.1), channel_id=1, source_target_pairs={{0,8},{1,9},{2,10},{3,11},{4,12},{5,13},{6,14},{7,15},{24,16},{25,... | collective-permute-start | bytes 786440 | tf_op jit(solution)/shard_map/ppermute | solution.py:173
  41.0 11.0 %collective-permute-start.17 = (bf16[128,1024]{1,0:T(8,128)(2,1)S(1)}, bf16[128,1024]{1,0:T(8,128)(2,1)S(1)}, u32[]{:S(2)}, u32[]{:S(2)}) collective-permute-start(bf16[128,1024]{1,0:T(8,128)(2,1)S(1)} %get-tuple-element.30.once_s.refs_3_), channel_id=1, source_target_pairs={{0,1},{1,0},{2,3},{3,2},{4,5},{5,4},{6,7},{7,6},{8,9},{9,8},{10,11... | collective-permute-start | bytes 786440 | tf_op jit(solution)/shard_map/ppermute | solution.py:173
  43.2 9.6 %collective-permute-start.16 = (bf16[512,128]{1,0:T(8,128)(2,1)S(1)}, bf16[512,128]{1,0:T(8,128)(2,1)S(1)}, u32[]{:S(2)}, u32[]{:S(2)}) collective-permute-start(bf16[512,128]{1,0:T(8,128)(2,1)S(1)} %get-tuple-element.38.sent), channel_id=1, source_target_pairs={{0,1},{1,0},{2,3},{3,2},{4,5},{5,4},{6,7},{7,6},{8,9},{9,8},{10,11... | collective-permute-start | bytes 393224 | tf_op jit(solution)/shard_map/ppermute | solution.py:173
  45.7 8.7 %collective-permute-start.21 = (bf16[128,1024]{1,0:T(8,128)(2,1)S(1)}, bf16[128,1024]{1,0:T(8,128)(2,1)S(1)}, u32[]{:S(2)}, u32[]{:S(2)}) collective-permute-start(bf16[128,1024]{1,0:T(8,128)(2,1)S(1)} %collective-permute-done.20.refs_5_), channel_id=1, source_target_pairs={{0,1},{1,0},{2,3},{3,2},{4,5},{5,4},{6,7},{7,6},{8,9},{9,8},{10,11... | collective-permute-start | bytes 786440 | tf_op jit(solution)/shard_map/ppermute | solution.py:173
  46.9 9.0 %collective-permute-start.23 = (bf16[128,1024]{1,0:T(8,128)(2,1)S(1)}, bf16[128,1024]{1,0:T(8,128)(2,1)S(1)}, u32[]{:S(2)}, u32[]{:S(2)}) collective-permute-start(bf16[128,1024]{1,0:T(8,128)(2,1)S(1)} %collective-permute-done.22.refs_7_), channel_id=1, source_target_pairs={{0,1},{1,0},{2,3},{3,2},{4,5},{5,4},{6,7},{7,6},{8,9},{9,8},{10,11... | collective-permute-start | bytes 786440 | tf_op jit(solution)/shard_map/ppermute | solution.py:173
  48.4 15.7 %collective-permute-start.24 = (bf16[128,1024]{1,0:T(8,128)(2,1)S(1)}, bf16[128,1024]{1,0:T(8,128)(2,1)S(1)}, u32[]{:S(2)}, u32[]{:S(2)}) collective-permute-start(bf16[128,1024]{1,0:T(8,128)(2,1)S(1)} %shard_map.37), channel_id=1, source_target_pairs={{0,16},{1,17},{2,18},{3,19},{4,20},{5,21},{6,22},{7,23},{24,0},{25... | collective-permute-start | bytes 786440 | tf_op jit(solution)/shard_map/ppermute | solution.py:173
  52.0 12.1 %collective-permute-start.28 = (bf16[128,1024]{1,0:T(8,128)(2,1)S(1)}, bf16[128,1024]{1,0:T(8,128)(2,1)S(1)}, u32[]{:S(2)}, u32[]{:S(2)}) collective-permute-start(bf16[128,1024]{1,0:T(8,128)(2,1)S(1)} %shard_map.38), channel_id=1, source_target_pairs={{0,8},{1,9},{2,10},{3,11},{4,12},{5,13},{6,14},{7,15},{24,16},{25,... | collective-permute-start | bytes 786440 | tf_op jit(solution)/shard_map/ppermute | solution.py:173
  53.1 10.9 %collective-permute-start.25 = (bf16[128,1024]{1,0:T(8,128)(2,1)S(1)}, bf16[128,1024]{1,0:T(8,128)(2,1)S(1)}, u32[]{:S(2)}, u32[]{:S(2)}) collective-permute-start(bf16[128,1024]{1,0:T(8,128)(2,1)S(1)} %get-tuple-element.42), channel_id=1, source_target_pairs={{0,6},{1,7},{2,4},{3,5},{4,2},{5,3},{6,0},{7,1},{8,14},{9,15},{10,... | collective-permute-start | bytes 786440 | tf_op jit(solution)/shard_map/ppermute | solution.py:173
  54.4 8.4 %collective-permute-start.18 = (bf16[128,256]{1,0:T(8,128)(2,1)S(1)}, bf16[128,256]{1,0:T(8,128)(2,1)S(1)}, u32[]{:S(2)}, u32[]{:S(2)}) collective-permute-start(bf16[128,256]{1,0:T(8,128)(2,1)S(1)} %get-tuple-element.40), channel_id=1, source_target_pairs={{0,2},{1,3},{2,0},{3,1},{4,6},{5,7},{6,4},{7,5},{8,10},{9,11},{10,... | collective-permute-start | bytes 196616 | tf_op jit(solution)/shard_map/ppermute | solution.py:173
  55.9 7.8 %collective-permute-start.19 = (bf16[128,256]{1,0:T(8,128)(2,1)S(1)}, bf16[128,256]{1,0:T(8,128)(2,1)S(1)}, u32[]{:S(2)}, u32[]{:S(2)}) collective-permute-start(bf16[128,256]{1,0:T(8,128)(2,1)S(1)} %get-tuple-element.41), channel_id=1, source_target_pairs={{0,4},{1,5},{2,6},{3,7},{4,0},{5,1},{6,2},{7,3},{8,12},{9,13},{10,... | collective-permute-start | bytes 196616 | tf_op jit(solution)/shard_map/ppermute | solution.py:173
where the time goes:
time: 65.3 us; the launch traced here: 65.2 us
  starting transfers between devices  27.2 us (42%)
  waiting for transfers between devices  27.1 us (42%)
  Pallas kernels  8.82 us (14%)
  local copies, waits for them, and re-layouts  1.92 us (3%)
    ppermute x29, starting transfers between devices, shift(): return lax.ppermute(x, axes, pairs)  27.2 us
    ppermute x29, waiting for transfers between devices, shift(): return lax.ppermute(x, axes, pairs)  27.1 us
    pallas_call x12, Pallas kernels, call(): pl.pallas_call(kernel, out_shape=outs, in_specs=[VM] * len(args), out_spe...  8.82 us
    unnamed x4, local copies, waits for them, and re-layouts  1.92 us
  transfers between devices with their start and end apart: 29, of which 13 were waited for; matrix products, arithmetic and copies ran while one was open for 0% of the time, Pallas kernels for 12%

commit v1 on v0

--- a/solution.py
+++ b/solution.py
@@ -105,20 +105,19 @@
     store_units(out_t, starts, raws[n:])
 
 
-def once_kernel(block_t, product, *refs):
-    *raws, kept, sent = refs
+def once_kernel(n_once, block_s, block_t, product, *refs):
+    raws, (kept, sent, *back) = refs[:n_once], refs[n_once:]
     stretch = 0.5 * block_t.shape[1] ** 0.5
     once_t = jnp.concatenate([unit_of(r[...]) for r in raws], axis=0)
     half = kept.shape[0]
+    sums = None
     for start, out in ((half, sent), (0, kept)):
         at = pl.ds(start, half)
         sim = product[at, :] - nt(block_t[at, :], once_t)
-        out[...] = jnp.tanh(stretch * sim).astype(BF16)
-
-
-def back_kernel(block_s, kept, sent, *back):
-    half = kept.shape[0]
-    sums = tn(kept[...], block_s[pl.ds(0, half), :]) + tn(sent[...], block_s[pl.ds(half, half), :])
+        part = jnp.tanh(stretch * sim).astype(BF16)
+        out[...] = part
+        term = tn(part, block_s[at, :])
+        sums = term if sums is None else sums + term
     rows = back[0].shape[0]
     for i, out in enumerate(back):
         out[...] = sums[i * rows : (i + 1) * rows].astype(BF16)
@@ -261,23 +260,16 @@
             flops=len(slots) * once_rows * work,
             into=(0, 1, 2),
         )
-    kept, sent = run(
-        once_kernel,
-        [shape(half, once_rows, BF16)] * 2,
+    kept, sent, *back = run(
+        functools.partial(once_kernel, n_once),
+        [shape(half, once_rows, BF16)] * 2 + [shape(rows, width, BF16)] * n_once,
+        block_s,
         block_t,
         product,
         *far_t[:n_once],
-        flops=n_gc * once_rows * work,
+        flops=2 * n_gc * once_rows * work,
     )
     came = across(sent, 1)
-    back = run(
-        back_kernel,
-        [shape(rows, width, BF16)] * n_once,
-        block_s,
-        kept,
-        sent,
-        flops=n_gc * once_rows * work,
-    )
     home = [along(b, n_gr - d) for b, d in zip(back, once)]
     n_pack = len(early)
     packed = run(

time: 65.3 us -> 65 us (level)
    pallas_call x12 -> x11, Pallas kernels: 8.82 us -> 8.79 us  [call(): pl.pallas_call(kernel, out_shape=outs, in_specs=[VM] * len(args), out_spe...]
    unnamed x4 -> x6, local copies, waits for them, and re-layouts: 1.92 us -> 1.93 us
where the time goes in v1:
time: 65 us; the launch traced here: 64.8 us
  starting transfers between devices  27.1 us (42%)
  waiting for transfers between devices  26.8 us (41%)
  Pallas kernels  8.79 us (14%)
  local copies, waits for them, and re-layouts  1.93 us (3%)
    ppermute x29, starting transfers between devices, shift(): return lax.ppermute(x, axes, pairs)  27.1 us
    ppermute x29, waiting for transfers between devices, shift(): return lax.ppermute(x, axes, pairs)  26.8 us
    pallas_call x11, Pallas kernels, call(): pl.pallas_call(kernel, out_shape=outs, in_specs=[VM] * len(args), out_spe...  8.79 us
    unnamed x6, local copies, waits for them, and re-layouts  1.93 us
  transfers between devices with their start and end apart: 29, of which 13 were waited for; matrix products, arithmetic and copies ran while one was open for 0% of the time, Pallas kernels for 12%

profile of v1, /device:TPU:0, one launch (start us, length us, event | category | flops | bytes accessed | tf_op | source)
XLA Modules:
  0.0 64.8 jit_solution(9043340589154772784)
XLA Ops:
  0.0 3.0 %collective-permute-start = (bf16[128,1024]{1,0:T(8,128)(2,1)}, bf16[128,1024]{1,0:T(8,128)(2,1)S(1)}, u32[]{:S(2)}, u32[]{:S(2)}) collective-permute-start(bf16[128,1024]{1,0:T(8,128)(2,1)} %student.1), channel_id=1, source_target_pairs={{0,2},{1,3},{2,0},{3,1},{4,6},{5,7},{6,4},{7,5},{8,10},{9,11},{10,... | collective-permute-start | bytes 786440 | tf_op jit(solution)/shard_map/ppermute | solution.py:172
  3.0 1.5 %collective-permute-start.1 = (bf16[128,1024]{1,0:T(8,128)(2,1)}, bf16[128,1024]{1,0:T(8,128)(2,1)S(1)}, u32[]{:S(2)}, u32[]{:S(2)}) collective-permute-start(bf16[128,1024]{1,0:T(8,128)(2,1)} %student.1), channel_id=1, source_target_pairs={{0,4},{1,5},{2,6},{3,7},{4,0},{5,1},{6,2},{7,3},{8,12},{9,13},{10,... | collective-permute-start | bytes 786440 | tf_op jit(solution)/shard_map/ppermute | solution.py:172
  5.0 4.1 %collective-permute-start.4 = (bf16[128,1024]{1,0:T(8,128)(2,1)}, bf16[128,1024]{1,0:T(8,128)(2,1)S(1)}, u32[]{:S(2)}, u32[]{:S(2)}) collective-permute-start(bf16[128,1024]{1,0:T(8,128)(2,1)} %student.1), channel_id=1, source_target_pairs={{0,24},{1,25},{2,26},{3,27},{4,28},{5,29},{6,30},{7,31},{24,8},{25... | collective-permute-start | bytes 786440 | tf_op jit(solution)/shard_map/ppermute | solution.py:172
  9.1 1.2 %collective-permute-done.refs_0_ = bf16[128,1024]{1,0:T(8,128)(2,1)S(1)} collective-permute-done((bf16[128,1024]{1,0:T(8,128)(2,1)}, bf16[128,1024]{1,0:T(8,128)(2,1)S(1)}, u32[]{:S(2)}, u32[]{:S(2)}) %collective-permute-start) | collective-permute-done | bytes 262176 | tf_op jit(solution)/shard_map/ppermute | solution.py:172
  10.3 2.0 %collective-permute-done.1.refs_1_ = bf16[128,1024]{1,0:T(8,128)(2,1)S(1)} collective-permute-done((bf16[128,1024]{1,0:T(8,128)(2,1)}, bf16[128,1024]{1,0:T(8,128)(2,1)S(1)}, u32[]{:S(2)}, u32[]{:S(2)}) %collective-permute-start.1) | collective-permute-done | bytes 262176 | tf_op jit(solution)/shard_map/ppermute | solution.py:172
  12.4 2.7 %collective-permute-done.2.refs_2_ = bf16[128,1024]{1,0:T(8,128)(2,1)S(1)} collective-permute-done((bf16[128,1024]{1,0:T(8,128)(2,1)}, bf16[128,1024]{1,0:T(8,128)(2,1)S(1)}, u32[]{:S(2)}, u32[]{:S(2)}) %collective-permute-start.2) | collective-permute-done | bytes 262176 | tf_op jit(solution)/shard_map/ppermute | solution.py:172
  15.1 3.9 %collective-permute-start.15 = (bf16[128,1024]{1,0:T(8,128)(2,1)}, bf16[128,1024]{1,0:T(8,128)(2,1)S(1)}, u32[]{:S(2)}, u32[]{:S(2)}) collective-permute-start(bf16[128,1024]{1,0:T(8,128)(2,1)} %teacher.1), channel_id=1, source_target_pairs={{0,24},{1,25},{2,26},{3,27},{4,28},{5,29},{6,30},{7,31},{24,8},{25... | collective-permute-start | bytes 786440 | tf_op jit(solution)/shard_map/ppermute | solution.py:172
  19.0 6.9 %collective-permute-done.4.refs_0_ = bf16[128,1024]{1,0:T(8,128)(2,1)S(1)} collective-permute-done((bf16[128,1024]{1,0:T(8,128)(2,1)}, bf16[128,1024]{1,0:T(8,128)(2,1)S(1)}, u32[]{:S(2)}, u32[]{:S(2)}) %collective-permute-start.4) | collective-permute-done | bytes 262176 | tf_op jit(solution)/shard_map/ppermute | solution.py:172
  25.8 1.6 %collective-permute-start.11 = (bf16[128,1024]{1,0:T(8,128)(2,1)S(1)}, bf16[128,1024]{1,0:T(8,128)(2,1)S(1)}, u32[]{:S(2)}, u32[]{:S(2)}) collective-permute-start(bf16[128,1024]{1,0:T(8,128)(2,1)S(1)} %collective-permute-done.refs_0_), channel_id=1, source_target_pairs={{0,4},{1,5},{2,6},{3,7},{4,0},{5,1},{6,2},{7,3},{8,12},{9,13},{10,... | collective-permute-start | bytes 786440 | tf_op jit(solution)/shard_map/ppermute | solution.py:172
  27.4 1.5 %collective-permute-start.13 = (bf16[128,1024]{1,0:T(8,128)(2,1)S(1)}, bf16[128,1024]{1,0:T(8,128)(2,1)S(1)}, u32[]{:S(2)}, u32[]{:S(2)}) collective-permute-start(bf16[128,1024]{1,0:T(8,128)(2,1)S(1)} %collective-permute-done.3.refs_3_), channel_id=1, source_target_pairs={{0,2},{1,3},{2,0},{3,1},{4,6},{5,7},{6,4},{7,5},{8,10},{9,11},{10,... | collective-permute-start | bytes 786440 | tf_op jit(solution)/shard_map/ppermute | solution.py:172
  28.9 1.4 %collective-permute-done.15.refs_0_ = bf16[128,1024]{1,0:T(8,128)(2,1)S(1)} collective-permute-done((bf16[128,1024]{1,0:T(8,128)(2,1)}, bf16[128,1024]{1,0:T(8,128)(2,1)S(1)}, u32[]{:S(2)}, u32[]{:S(2)}) %collective-permute-start.15) | collective-permute-done | bytes 262176 | tf_op jit(solution)/shard_map/ppermute | solution.py:172
  30.9 1.3 %collective-permute-done.11.refs_0_ = bf16[128,1024]{1,0:T(8,128)(2,1)S(1)} collective-permute-done((bf16[128,1024]{1,0:T(8,128)(2,1)S(1)}, bf16[128,1024]{1,0:T(8,128)(2,1)S(1)}, u32[]{:S(2)}, u32[]{:S(2)}) %collective-permute-start.11) | collective-permute-done | bytes 262176 | tf_op jit(solution)/shard_map/ppermute | solution.py:172
  32.2 1.6 %collective-permute-done.13.refs_2_ = bf16[128,1024]{1,0:T(8,128)(2,1)S(1)} collective-permute-done((bf16[128,1024]{1,0:T(8,128)(2,1)S(1)}, bf16[128,1024]{1,0:T(8,128)(2,1)S(1)}, u32[]{:S(2)}, u32[]{:S(2)}) %collective-permute-start.13) | collective-permute-done | bytes 262176 | tf_op jit(solution)/shard_map/ppermute | solution.py:172
  33.8 1.0 %copy-done = bf16[128,1024]{1,0:T(8,128)(2,1)S(1)} copy-done((bf16[128,1024]{1,0:T(8,128)(2,1)S(1)}, bf16[128,1024]{1,0:T(8,128)(2,1)}, u32[]{:S(2)}) %copy-start) | copy-done | bytes 262168
  34.8 0.9 %copy-done.1 = bf16[128,1024]{1,0:T(8,128)(2,1)S(1)} copy-done((bf16[128,1024]{1,0:T(8,128)(2,1)S(1)}, bf16[128,1024]{1,0:T(8,128)(2,1)}, u32[]{:S(2)}) %copy-start.1) | copy-done | bytes 262168
  36.9 1.6 %collective-permute-start.20 = (bf16[128,1024]{1,0:T(8,128)(2,1)S(1)}, bf16[128,1024]{1,0:T(8,128)(2,1)S(1)}, u32[]{:S(2)}, u32[]{:S(2)}) collective-permute-start(bf16[128,1024]{1,0:T(8,128)(2,1)S(1)} %get-tuple-element.31.once_s.refs_3_), channel_id=1, source_target_pairs={{0,2},{1,3},{2,0},{3,1},{4,6},{5,7},{6,4},{7,5},{8,10},{9,11},{10,... | collective-permute-start | bytes 786440 | tf_op jit(solution)/shard_map/ppermute | solution.py:172
  39.0 2.0 %collective-permute-start.27 = (bf16[128,1024]{1,0:T(8,128)(2,1)S(1)}, bf16[128,1024]{1,0:T(8,128)(2,1)S(1)}, u32[]{:S(2)}, u32[]{:S(2)}) collective-permute-start(bf16[128,1024]{1,0:T(8,128)(2,1)S(1)} %copy-done.2), channel_id=1, source_target_pairs={{0,8},{1,9},{2,10},{3,11},{4,12},{5,13},{6,14},{7,15},{24,16},{25,... | collective-permute-start | bytes 786440 | tf_op jit(solution)/shard_map/ppermute | solution.py:172
  41.0 0.7 %shard_map.31 = (bf16[1024,1024]{1,0:T(8,128)(2,1)S(1)}, bf16[1024,1024]{1,0:T(8,128)(2,1)S(1)}, f32[1024,128]{1,0:T(8,128)S(1)}) custom-call(bf16[1024,1024]{1,0:T(8,128)(2,1)S(1)} %get-tuple-element.28.block_s, bf16[1024,1024]{1,0:T(8,128)(2,1)S(1)} %get-tuple-element.29.block_t, ...), custom_call_target="tpu_custom_call", output_to_operand_aliasing={{0}: (0, {}), {1}: (1, {}), {2}: (2, {})} | custom-call | flops 100663296 | bytes 11272192 | tf_op jit(solution)/shard_map/pallas_call | solution.py:39
  42.1 1.3 %shard_map.34 = (bf16[512,128]{1,0:T(8,128)(2,1)S(1)}, bf16[512,128]{1,0:T(8,128)(2,1)S(1)}, bf16[128,1024]{1,0:T(8,128)(2,1)S(1)}) custom-call(bf16[1024,1024]{1,0:T(8,128)(2,1)S(1)} %get-tuple-element.35.block_s, bf16[1024,1024]{1,0:T(8,128)(2,1)S(1)} %get-tuple-element.36.block_t, f32[1024,128]{1,0:T(8,128)S(1)} %get-tuple-element.37.product, ...), custom_call_target="tpu_custom_call" | custom-call | flops 536870912 | bytes 5505024 | tf_op jit(solution)/shard_map/pallas_call | solution.py:39
  43.4 0.6 collective-permute-start.16
  44.0 1.7 %collective-permute-done.20.refs_5_ = bf16[128,1024]{1,0:T(8,128)(2,1)S(1)} collective-permute-done((bf16[128,1024]{1,0:T(8,128)(2,1)S(1)}, bf16[128,1024]{1,0:T(8,128)(2,1)S(1)}, u32[]{:S(2)}, u32[]{:S(2)}) %collective-permute-start.20) | collective-permute-done | bytes 262176 | tf_op jit(solution)/shard_map/ppermute | solution.py:172
  45.7 1.2 %collective-permute-done.22.refs_7_ = bf16[128,1024]{1,0:T(8,128)(2,1)S(1)} collective-permute-done((bf16[128,1024]{1,0:T(8,128)(2,1)S(1)}, bf16[128,1024]{1,0:T(8,128)(2,1)S(1)}, u32[]{:S(2)}, u32[]{:S(2)}) %collective-permute-start.22) | collective-permute-done | bytes 262176 | tf_op jit(solution)/shard_map/ppermute | solution.py:172
  46.9 1.5 %collective-permute-done.27.refs_1_ = bf16[128,1024]{1,0:T(8,128)(2,1)S(1)} collective-permute-done((bf16[128,1024]{1,0:T(8,128)(2,1)S(1)}, bf16[128,1024]{1,0:T(8,128)(2,1)S(1)}, u32[]{:S(2)}, u32[]{:S(2)}) %collective-permute-start.27) | collective-permute-done | bytes 262176 | tf_op jit(solution)/shard_map/ppermute | solution.py:172
  48.4 1.7 %collective-permute-start.24 = (bf16[128,1024]{1,0:T(8,128)(2,1)S(1)}, bf16[128,1024]{1,0:T(8,128)(2,1)S(1)}, u32[]{:S(2)}, u32[]{:S(2)}) collective-permute-start(bf16[128,1024]{1,0:T(8,128)(2,1)S(1)} %get-tuple-element.43), channel_id=1, source_target_pairs={{0,16},{1,17},{2,18},{3,19},{4,20},{5,21},{6,22},{7,23},{24,0},{25... | collective-permute-start | bytes 786440 | tf_op jit(solution)/shard_map/ppermute | solution.py:172
  50.1 1.9 %shard_map.37 = bf16[128,1024]{1,0:T(8,128)(2,1)S(1)} custom-call(bf16[1024,1024]{1,0:T(8,128)(2,1)S(1)} %get-tuple-element.35.block_s, bf16[1024,1024]{1,0:T(8,128)(2,1)S(1)} %get-tuple-element.36.block_t, bf16[128,1024]{1,0:T(8,128)(2,1)S(1)} %collective-permute-done.26.refs_0_, bf16[128,1024]{1,0:T(8,128)(2,1)S(1)} %collective-permute-done.27.refs_1_), custom_call_target="tpu_custom_call" | custom-call | flops 805306368 | bytes 4980736 | tf_op jit(solution)/shard_map/pallas_call | solution.py:39
  52.0 0.6 collective-permute-start.28
  52.8 1.6 %collective-permute-start.25 = (bf16[128,1024]{1,0:T(8,128)(2,1)S(1)}, bf16[128,1024]{1,0:T(8,128)(2,1)S(1)}, u32[]{:S(2)}, u32[]{:S(2)}) collective-permute-start(bf16[128,1024]{1,0:T(8,128)(2,1)S(1)} %get-tuple-element.44), channel_id=1, source_target_pairs={{0,6},{1,7},{2,4},{3,5},{4,2},{5,3},{6,0},{7,1},{8,14},{9,15},{10,... | collective-permute-start | bytes 786440 | tf_op jit(solution)/shard_map/ppermute | solution.py:172
  54.4 1.5 %collective-permute-start.18 = (bf16[128,256]{1,0:T(8,128)(2,1)S(1)}, bf16[128,256]{1,0:T(8,128)(2,1)S(1)}, u32[]{:S(2)}, u32[]{:S(2)}) collective-permute-start(bf16[128,256]{1,0:T(8,128)(2,1)S(1)} %get-tuple-element.41), channel_id=1, source_target_pairs={{0,2},{1,3},{2,0},{3,1},{4,6},{5,7},{6,4},{7,5},{8,10},{9,11},{10,... | collective-permute-start | bytes 196616 | tf_op jit(solution)/shard_map/ppermute | solution.py:172
  56.4 1.7 %shard_map.33.before = f32[128,1024]{1,0:T(8,128)S(1)} custom-call(bf16[128,1024]{1,0:T(8,128)(2,1)S(1)} %get-tuple-element.25.own_s, bf16[128,1024]{1,0:T(8,128)(2,1)S(1)} %get-tuple-element.27.own_t, bf16[1024,1024]{1,0:T(8,128)(2,1)S(1)} %get-tuple-element.35.block_s, bf16[1024,1024]{1,0:T(8,128)(2,1)S(1)} %get-tuple-element.36.block_t), custom_call_target="tpu_custom_call" | custom-call | flops 805306368 | bytes 5242880 | tf_op jit(solution)/shard_map/pallas_call | solution.py:39
  58.1 4.1 %collective-permute-done.18.refs_1_ = bf16[128,256]{1,0:T(8,128)(2,1)S(1)} collective-permute-done((bf16[128,256]{1,0:T(8,128)(2,1)S(1)}, bf16[128,256]{1,0:T(8,128)(2,1)S(1)}, u32[]{:S(2)}, u32[]{:S(2)}) %collective-permute-start.18) | collective-permute-done | bytes 65568 | tf_op jit(solution)/shard_map/ppermute | solution.py:172
  62.2 0.9 %collective-permute-done.19.refs_2_ = bf16[128,256]{1,0:T(8,128)(2,1)S(1)} collective-permute-done((bf16[128,256]{1,0:T(8,128)(2,1)S(1)}, bf16[128,256]{1,0:T(8,128)(2,1)S(1)}, u32[]{:S(2)}, u32[]{:S(2)}) %collective-permute-start.19) | collective-permute-done | bytes 65568 | tf_op jit(solution)/shard_map/ppermute | solution.py:172
  63.7 1.1 %shard_map.38 = f32[128,1024]{1,0:T(8,128)} custom-call(bf16[128,1024]{1,0:T(8,128)(2,1)S(1)} %get-tuple-element.25.own_s, f32[128,128]{1,0:T(8,128)S(1)} %get-tuple-element.26.scale, f32[128,1024]{1,0:T(8,128)S(1)} %shard_map.36.refs_0_, bf16[128,1024]{1,0:T(8,128)(2,1)S(1)} %collective-permute-done.24.refs_1_, ...), custom_call_target="tpu_custom_call" | custom-call | bytes 2162688 | tf_op jit(solution)/shard_map/pallas_call | solution.py:39
  (43 shorter events, 4.6 us)
Async XLA Ops:
  0.0 10.3 %collective-permute-start = (bf16[128,1024]{1,0:T(8,128)(2,1)}, bf16[128,1024]{1,0:T(8,128)(2,1)S(1)}, u32[]{:S(2)}, u32[]{:S(2)}) collective-permute-start(bf16[128,1024]{1,0:T(8,128)(2,1)} %student.1), channel_id=1, source_target_pairs={{0,2},{1,3},{2,0},{3,1},{4,6},{5,7},{6,4},{7,5},{8,10},{9,11},{10,... | collective-permute-start | bytes 786440 | tf_op jit(solution)/shard_map/ppermute | solution.py:172
  3.0 9.4 %collective-permute-start.1 = (bf16[128,1024]{1,0:T(8,128)(2,1)}, bf16[128,1024]{1,0:T(8,128)(2,1)S(1)}, u32[]{:S(2)}, u32[]{:S(2)}) collective-permute-start(bf16[128,1024]{1,0:T(8,128)(2,1)} %student.1), channel_id=1, source_target_pairs={{0,4},{1,5},{2,6},{3,7},{4,0},{5,1},{6,2},{7,3},{8,12},{9,13},{10,... | collective-permute-start | bytes 786440 | tf_op jit(solution)/shard_map/ppermute | solution.py:172
  4.5 10.6 %collective-permute-start.2 = (bf16[128,1024]{1,0:T(8,128)(2,1)}, bf16[128,1024]{1,0:T(8,128)(2,1)S(1)}, u32[]{:S(2)}, u32[]{:S(2)}) collective-permute-start(bf16[128,1024]{1,0:T(8,128)(2,1)} %teacher.1), channel_id=1, source_target_pairs={{0,2},{1,3},{2,0},{3,1},{4,6},{5,7},{6,4},{7,5},{8,10},{9,11},{10,... | collective-permute-start | bytes 786440 | tf_op jit(solution)/shard_map/ppermute | solution.py:172
  5.0 13.9 %collective-permute-start.3 = (bf16[128,1024]{1,0:T(8,128)(2,1)}, bf16[128,1024]{1,0:T(8,128)(2,1)S(1)}, u32[]{:S(2)}, u32[]{:S(2)}) collective-permute-start(bf16[128,1024]{1,0:T(8,128)(2,1)} %teacher.1), channel_id=1, source_target_pairs={{0,4},{1,5},{2,6},{3,7},{4,0},{5,1},{6,2},{7,3},{8,12},{9,13},{10,... | collective-permute-start | bytes 786440 | tf_op jit(solution)/shard_map/ppermute | solution.py:172
  5.0 20.8 %collective-permute-start.4 = (bf16[128,1024]{1,0:T(8,128)(2,1)}, bf16[128,1024]{1,0:T(8,128)(2,1)S(1)}, u32[]{:S(2)}, u32[]{:S(2)}) collective-permute-start(bf16[128,1024]{1,0:T(8,128)(2,1)} %student.1), channel_id=1, source_target_pairs={{0,24},{1,25},{2,26},{3,27},{4,28},{5,29},{6,30},{7,31},{24,8},{25... | collective-permute-start | bytes 786440 | tf_op jit(solution)/shard_map/ppermute | solution.py:172
  10.3 17.1 %collective-permute-start.5 = (bf16[128,1024]{1,0:T(8,128)(2,1)}, bf16[128,1024]{1,0:T(8,128)(2,1)S(1)}, u32[]{:S(2)}, u32[]{:S(2)}) collective-permute-start(bf16[128,1024]{1,0:T(8,128)(2,1)} %student.1), channel_id=1, source_target_pairs={{0,1},{1,0},{2,3},{3,2},{4,5},{5,4},{6,7},{7,6},{8,9},{9,8},{10,11... | collective-permute-start | bytes 786440 | tf_op jit(solution)/shard_map/ppermute | solution.py:172
  12.4 16.6 %collective-permute-start.8 = (bf16[128,1024]{1,0:T(8,128)(2,1)}, bf16[128,1024]{1,0:T(8,128)(2,1)S(1)}, u32[]{:S(2)}, u32[]{:S(2)}) collective-permute-start(bf16[128,1024]{1,0:T(8,128)(2,1)} %teacher.1), channel_id=1, source_target_pairs={{0,1},{1,0},{2,3},{3,2},{4,5},{5,4},{6,7},{7,6},{8,9},{9,8},{10,11... | collective-permute-start | bytes 786440 | tf_op jit(solution)/shard_map/ppermute | solution.py:172
  15.1 15.3 %collective-permute-start.15 = (bf16[128,1024]{1,0:T(8,128)(2,1)}, bf16[128,1024]{1,0:T(8,128)(2,1)S(1)}, u32[]{:S(2)}, u32[]{:S(2)}) collective-permute-start(bf16[128,1024]{1,0:T(8,128)(2,1)} %teacher.1), channel_id=1, source_target_pairs={{0,24},{1,25},{2,26},{3,27},{4,28},{5,29},{6,30},{7,31},{24,8},{25... | collective-permute-start | bytes 786440 | tf_op jit(solution)/shard_map/ppermute | solution.py:172
  19.0 11.4 %collective-permute-start.6 = (bf16[128,1024]{1,0:T(8,128)(2,1)S(1)}, bf16[128,1024]{1,0:T(8,128)(2,1)S(1)}, u32[]{:S(2)}, u32[]{:S(2)}) collective-permute-start(bf16[128,1024]{1,0:T(8,128)(2,1)S(1)} %collective-permute-done.refs_0_), channel_id=1, source_target_pairs={{0,1},{1,0},{2,3},{3,2},{4,5},{5,4},{6,7},{7,6},{8,9},{9,8},{10,11... | collective-permute-start | bytes 786440 | tf_op jit(solution)/shard_map/ppermute | solution.py:172
  25.8 6.4 %collective-permute-start.11 = (bf16[128,1024]{1,0:T(8,128)(2,1)S(1)}, bf16[128,1024]{1,0:T(8,128)(2,1)S(1)}, u32[]{:S(2)}, u32[]{:S(2)}) collective-permute-start(bf16[128,1024]{1,0:T(8,128)(2,1)S(1)} %collective-permute-done.refs_0_), channel_id=1, source_target_pairs={{0,4},{1,5},{2,6},{3,7},{4,0},{5,1},{6,2},{7,3},{8,12},{9,13},{10,... | collective-permute-start | bytes 786440 | tf_op jit(solution)/shard_map/ppermute | solution.py:172
  27.4 6.4 %collective-permute-start.13 = (bf16[128,1024]{1,0:T(8,128)(2,1)S(1)}, bf16[128,1024]{1,0:T(8,128)(2,1)S(1)}, u32[]{:S(2)}, u32[]{:S(2)}) collective-permute-start(bf16[128,1024]{1,0:T(8,128)(2,1)S(1)} %collective-permute-done.3.refs_3_), channel_id=1, source_target_pairs={{0,2},{1,3},{2,0},{3,1},{4,6},{5,7},{6,4},{7,5},{8,10},{9,11},{10,... | collective-permute-start | bytes 786440 | tf_op jit(solution)/shard_map/ppermute | solution.py:172
  28.9 4.9 %collective-permute-start.7 = (bf16[128,1024]{1,0:T(8,128)(2,1)S(1)}, bf16[128,1024]{1,0:T(8,128)(2,1)S(1)}, u32[]{:S(2)}, u32[]{:S(2)}) collective-permute-start(bf16[128,1024]{1,0:T(8,128)(2,1)S(1)} %collective-permute-done.1.refs_1_), channel_id=1, source_target_pairs={{0,1},{1,0},{2,3},{3,2},{4,5},{5,4},{6,7},{7,6},{8,9},{9,8},{10,11... | collective-permute-start | bytes 786440 | tf_op jit(solution)/shard_map/ppermute | solution.py:172
  30.4 6.5 %collective-permute-start.9 = (bf16[128,1024]{1,0:T(8,128)(2,1)S(1)}, bf16[128,1024]{1,0:T(8,128)(2,1)S(1)}, u32[]{:S(2)}, u32[]{:S(2)}) collective-permute-start(bf16[128,1024]{1,0:T(8,128)(2,1)S(1)} %collective-permute-done.2.refs_2_), channel_id=1, source_target_pairs={{0,1},{1,0},{2,3},{3,2},{4,5},{5,4},{6,7},{7,6},{8,9},{9,8},{10,11... | collective-permute-start | bytes 786440 | tf_op jit(solution)/shard_map/ppermute | solution.py:172
  30.4 8.1 %collective-permute-start.10 = (bf16[128,1024]{1,0:T(8,128)(2,1)S(1)}, bf16[128,1024]{1,0:T(8,128)(2,1)S(1)}, u32[]{:S(2)}, u32[]{:S(2)}) collective-permute-start(bf16[128,1024]{1,0:T(8,128)(2,1)S(1)} %collective-permute-done.3.refs_3_), channel_id=1, source_target_pairs={{0,1},{1,0},{2,3},{3,2},{4,5},{5,4},{6,7},{7,6},{8,9},{9,8},{10,11... | collective-permute-start | bytes 786440 | tf_op jit(solution)/shard_map/ppermute | solution.py:172
  32.2 6.8 %collective-permute-start.12 = (bf16[128,1024]{1,0:T(8,128)(2,1)S(1)}, bf16[128,1024]{1,0:T(8,128)(2,1)S(1)}, u32[]{:S(2)}, u32[]{:S(2)}) collective-permute-start(bf16[128,1024]{1,0:T(8,128)(2,1)S(1)} %collective-permute-done.11.refs_0_), channel_id=1, source_target_pairs={{0,1},{1,0},{2,3},{3,2},{4,5},{5,4},{6,7},{7,6},{8,9},{9,8},{10,11... | collective-permute-start | bytes 786440 | tf_op jit(solution)/shard_map/ppermute | solution.py:172
  33.8 7.2 %collective-permute-start.14 = (bf16[128,1024]{1,0:T(8,128)(2,1)S(1)}, bf16[128,1024]{1,0:T(8,128)(2,1)S(1)}, u32[]{:S(2)}, u32[]{:S(2)}) collective-permute-start(bf16[128,1024]{1,0:T(8,128)(2,1)S(1)} %collective-permute-done.13.refs_2_), channel_id=1, source_target_pairs={{0,1},{1,0},{2,3},{3,2},{4,5},{5,4},{6,7},{7,6},{8,9},{9,8},{10,11... | collective-permute-start | bytes 786440 | tf_op jit(solution)/shard_map/ppermute | solution.py:172
  33.8 9.6 %collective-permute-start.26 = (bf16[128,1024]{1,0:T(8,128)(2,1)}, bf16[128,1024]{1,0:T(8,128)(2,1)S(1)}, u32[]{:S(2)}, u32[]{:S(2)}) collective-permute-start(bf16[128,1024]{1,0:T(8,128)(2,1)} %student.1), channel_id=1, source_target_pairs={{0,8},{1,9},{2,10},{3,11},{4,12},{5,13},{6,14},{7,15},{24,16},{25,... | collective-permute-start | bytes 786440 | tf_op jit(solution)/shard_map/ppermute | solution.py:172
  33.8 1.0 %copy-start = (bf16[128,1024]{1,0:T(8,128)(2,1)S(1)}, bf16[128,1024]{1,0:T(8,128)(2,1)}, u32[]{:S(2)}) copy-start(bf16[128,1024]{1,0:T(8,128)(2,1)} %student.1) | copy-start | bytes 786436
  34.8 0.9 %copy-start.1 = (bf16[128,1024]{1,0:T(8,128)(2,1)S(1)}, bf16[128,1024]{1,0:T(8,128)(2,1)}, u32[]{:S(2)}) copy-start(bf16[128,1024]{1,0:T(8,128)(2,1)} %teacher.1) | copy-start | bytes 786436
  36.0 3.0 %copy-start.2 = (bf16[128,1024]{1,0:T(8,128)(2,1)S(1)}, bf16[128,1024]{1,0:T(8,128)(2,1)}, u32[]{:S(2)}) copy-start(bf16[128,1024]{1,0:T(8,128)(2,1)} %teacher.1) | copy-start | bytes 786436
  36.9 8.8 %collective-permute-start.20 = (bf16[128,1024]{1,0:T(8,128)(2,1)S(1)}, bf16[128,1024]{1,0:T(8,128)(2,1)S(1)}, u32[]{:S(2)}, u32[]{:S(2)}) collective-permute-start(bf16[128,1024]{1,0:T(8,128)(2,1)S(1)} %get-tuple-element.31.once_s.refs_3_), channel_id=1, source_target_pairs={{0,2},{1,3},{2,0},{3,1},{4,6},{5,7},{6,4},{7,5},{8,10},{9,11},{10,... | collective-permute-start | bytes 786440 | tf_op jit(solution)/shard_map/ppermute | solution.py:172
  38.4 8.4 %collective-permute-start.22 = (bf16[128,1024]{1,0:T(8,128)(2,1)S(1)}, bf16[128,1024]{1,0:T(8,128)(2,1)S(1)}, u32[]{:S(2)}, u32[]{:S(2)}) collective-permute-start(bf16[128,1024]{1,0:T(8,128)(2,1)S(1)} %get-tuple-element.31.once_s.refs_3_), channel_id=1, source_target_pairs={{0,4},{1,5},{2,6},{3,7},{4,0},{5,1},{6,2},{7,3},{8,12},{9,13},{10,... | collective-permute-start | bytes 786440 | tf_op jit(solution)/shard_map/ppermute | solution.py:172
  39.0 9.4 %collective-permute-start.27 = (bf16[128,1024]{1,0:T(8,128)(2,1)S(1)}, bf16[128,1024]{1,0:T(8,128)(2,1)S(1)}, u32[]{:S(2)}, u32[]{:S(2)}) collective-permute-start(bf16[128,1024]{1,0:T(8,128)(2,1)S(1)} %copy-done.2), channel_id=1, source_target_pairs={{0,8},{1,9},{2,10},{3,11},{4,12},{5,13},{6,14},{7,15},{24,16},{25,... | collective-permute-start | bytes 786440 | tf_op jit(solution)/shard_map/ppermute | solution.py:172
  41.0 11.0 %collective-permute-start.17 = (bf16[128,1024]{1,0:T(8,128)(2,1)S(1)}, bf16[128,1024]{1,0:T(8,128)(2,1)S(1)}, u32[]{:S(2)}, u32[]{:S(2)}) collective-permute-start(bf16[128,1024]{1,0:T(8,128)(2,1)S(1)} %get-tuple-element.31.once_s.refs_3_), channel_id=1, source_target_pairs={{0,1},{1,0},{2,3},{3,2},{4,5},{5,4},{6,7},{7,6},{8,9},{9,8},{10,11... | collective-permute-start | bytes 786440 | tf_op jit(solution)/shard_map/ppermute | solution.py:172
  43.4 9.1 %collective-permute-start.16 = (bf16[512,128]{1,0:T(8,128)(2,1)S(1)}, bf16[512,128]{1,0:T(8,128)(2,1)S(1)}, u32[]{:S(2)}, u32[]{:S(2)}) collective-permute-start(bf16[512,128]{1,0:T(8,128)(2,1)S(1)} %get-tuple-element.39), channel_id=1, source_target_pairs={{0,1},{1,0},{2,3},{3,2},{4,5},{5,4},{6,7},{7,6},{8,9},{9,8},{10,11... | collective-permute-start | bytes 393224 | tf_op jit(solution)/shard_map/ppermute | solution.py:172
  45.7 8.7 %collective-permute-start.21 = (bf16[128,1024]{1,0:T(8,128)(2,1)S(1)}, bf16[128,1024]{1,0:T(8,128)(2,1)S(1)}, u32[]{:S(2)}, u32[]{:S(2)}) collective-permute-start(bf16[128,1024]{1,0:T(8,128)(2,1)S(1)} %collective-permute-done.20.refs_5_), channel_id=1, source_target_pairs={{0,1},{1,0},{2,3},{3,2},{4,5},{5,4},{6,7},{7,6},{8,9},{9,8},{10,11... | collective-permute-start | bytes 786440 | tf_op jit(solution)/shard_map/ppermute | solution.py:172
  46.9 9.0 %collective-permute-start.23 = (bf16[128,1024]{1,0:T(8,128)(2,1)S(1)}, bf16[128,1024]{1,0:T(8,128)(2,1)S(1)}, u32[]{:S(2)}, u32[]{:S(2)}) collective-permute-start(bf16[128,1024]{1,0:T(8,128)(2,1)S(1)} %collective-permute-done.22.refs_7_), channel_id=1, source_target_pairs={{0,1},{1,0},{2,3},{3,2},{4,5},{5,4},{6,7},{7,6},{8,9},{9,8},{10,11... | collective-permute-start | bytes 786440 | tf_op jit(solution)/shard_map/ppermute | solution.py:172
  48.4 15.2 %collective-permute-start.24 = (bf16[128,1024]{1,0:T(8,128)(2,1)S(1)}, bf16[128,1024]{1,0:T(8,128)(2,1)S(1)}, u32[]{:S(2)}, u32[]{:S(2)}) collective-permute-start(bf16[128,1024]{1,0:T(8,128)(2,1)S(1)} %get-tuple-element.43), channel_id=1, source_target_pairs={{0,16},{1,17},{2,18},{3,19},{4,20},{5,21},{6,22},{7,23},{24,0},{25... | collective-permute-start | bytes 786440 | tf_op jit(solution)/shard_map/ppermute | solution.py:172
  52.0 11.8 %collective-permute-start.28 = (bf16[128,1024]{1,0:T(8,128)(2,1)S(1)}, bf16[128,1024]{1,0:T(8,128)(2,1)S(1)}, u32[]{:S(2)}, u32[]{:S(2)}) collective-permute-start(bf16[128,1024]{1,0:T(8,128)(2,1)S(1)} %shard_map.37), channel_id=1, source_target_pairs={{0,8},{1,9},{2,10},{3,11},{4,12},{5,13},{6,14},{7,15},{24,16},{25,... | collective-permute-start | bytes 786440 | tf_op jit(solution)/shard_map/ppermute | solution.py:172
  52.8 10.9 %collective-permute-start.25 = (bf16[128,1024]{1,0:T(8,128)(2,1)S(1)}, bf16[128,1024]{1,0:T(8,128)(2,1)S(1)}, u32[]{:S(2)}, u32[]{:S(2)}) collective-permute-start(bf16[128,1024]{1,0:T(8,128)(2,1)S(1)} %get-tuple-element.44), channel_id=1, source_target_pairs={{0,6},{1,7},{2,4},{3,5},{4,2},{5,3},{6,0},{7,1},{8,14},{9,15},{10,... | collective-permute-start | bytes 786440 | tf_op jit(solution)/shard_map/ppermute | solution.py:172
  54.4 7.8 %collective-permute-start.18 = (bf16[128,256]{1,0:T(8,128)(2,1)S(1)}, bf16[128,256]{1,0:T(8,128)(2,1)S(1)}, u32[]{:S(2)}, u32[]{:S(2)}) collective-permute-start(bf16[128,256]{1,0:T(8,128)(2,1)S(1)} %get-tuple-element.41), channel_id=1, source_target_pairs={{0,2},{1,3},{2,0},{3,1},{4,6},{5,7},{6,4},{7,5},{8,10},{9,11},{10,... | collective-permute-start | bytes 196616 | tf_op jit(solution)/shard_map/ppermute | solution.py:172
  55.9 7.2 %collective-permute-start.19 = (bf16[128,256]{1,0:T(8,128)(2,1)S(1)}, bf16[128,256]{1,0:T(8,128)(2,1)S(1)}, u32[]{:S(2)}, u32[]{:S(2)}) collective-permute-start(bf16[128,256]{1,0:T(8,128)(2,1)S(1)} %get-tuple-element.42), channel_id=1, source_target_pairs={{0,4},{1,5},{2,6},{3,7},{4,0},{5,1},{6,2},{7,3},{8,12},{9,13},{10,... | collective-permute-start | bytes 196616 | tf_op jit(solution)/shard_map/ppermute | solution.py:172

commit v2 on v1

--- a/solution.py
+++ b/solution.py
@@ -58,14 +58,8 @@
 
 def pull_of(rows_s, rows_t, block_s, block_t):
     stretch = 0.5 * rows_s.shape[1] ** 0.5
-    total = None
-    half = block_s.shape[0] // 2
-    for i in range(2):
-        at = pl.ds(i * half, half)
-        sim = nt(block_s[at, :], rows_s) - nt(block_t[at, :], rows_t)
-        term = tn(jnp.tanh(stretch * sim).astype(BF16), block_s[at, :])
-        total = term if total is None else total + term
-    return total
+    sim = nt(block_s[...], rows_s) - nt(block_t[...], rows_t)
+    return tn(jnp.tanh(stretch * sim).astype(BF16), block_s[...])
 
 
 def own_kernel(student, teacher, unit_s, unit_t, scale):

time: 65 us -> 65 us (level)
  no operation moved by 1% of the time
where the time goes in v2:
time: 65 us; the launch traced here: 64.8 us
  starting transfers between devices  27.1 us (42%)
  waiting for transfers between devices  27 us (42%)
  Pallas kernels  8.64 us (13%)
  local copies, waits for them, and re-layouts  1.93 us (3%)
    ppermute x29, starting transfers between devices, shift(): return lax.ppermute(x, axes, pairs)  27.1 us
    ppermute x29, waiting for transfers between devices, shift(): return lax.ppermute(x, axes, pairs)  27 us
    pallas_call x11, Pallas kernels, call(): pl.pallas_call(kernel, out_shape=outs, in_specs=[VM] * len(args), out_spe...  8.64 us
    unnamed x6, local copies, waits for them, and re-layouts  1.93 us
  transfers between devices with their start and end apart: 29, of which 13 were waited for; matrix products, arithmetic and copies ran while one was open for 0% of the time, Pallas kernels for 12%

profile of v2, /device:TPU:0, one launch (start us, length us, event | category | flops | bytes accessed | tf_op | source)
XLA Modules:
  0.0 64.8 jit_solution(16373420629894253905)
XLA Ops:
  0.0 3.0 %collective-permute-start = (bf16[128,1024]{1,0:T(8,128)(2,1)}, bf16[128,1024]{1,0:T(8,128)(2,1)S(1)}, u32[]{:S(2)}, u32[]{:S(2)}) collective-permute-start(bf16[128,1024]{1,0:T(8,128)(2,1)} %student.1), channel_id=1, source_target_pairs={{0,2},{1,3},{2,0},{3,1},{4,6},{5,7},{6,4},{7,5},{8,10},{9,11},{10,... | collective-permute-start | bytes 786440 | tf_op jit(solution)/shard_map/ppermute | solution.py:166
  3.0 1.5 %collective-permute-start.1 = (bf16[128,1024]{1,0:T(8,128)(2,1)}, bf16[128,1024]{1,0:T(8,128)(2,1)S(1)}, u32[]{:S(2)}, u32[]{:S(2)}) collective-permute-start(bf16[128,1024]{1,0:T(8,128)(2,1)} %student.1), channel_id=1, source_target_pairs={{0,4},{1,5},{2,6},{3,7},{4,0},{5,1},{6,2},{7,3},{8,12},{9,13},{10,... | collective-permute-start | bytes 786440 | tf_op jit(solution)/shard_map/ppermute | solution.py:166
  5.0 4.1 %collective-permute-start.4 = (bf16[128,1024]{1,0:T(8,128)(2,1)}, bf16[128,1024]{1,0:T(8,128)(2,1)S(1)}, u32[]{:S(2)}, u32[]{:S(2)}) collective-permute-start(bf16[128,1024]{1,0:T(8,128)(2,1)} %student.1), channel_id=1, source_target_pairs={{0,24},{1,25},{2,26},{3,27},{4,28},{5,29},{6,30},{7,31},{24,8},{25... | collective-permute-start | bytes 786440 | tf_op jit(solution)/shard_map/ppermute | solution.py:166
  9.1 1.2 %collective-permute-done.refs_0_ = bf16[128,1024]{1,0:T(8,128)(2,1)S(1)} collective-permute-done((bf16[128,1024]{1,0:T(8,128)(2,1)}, bf16[128,1024]{1,0:T(8,128)(2,1)S(1)}, u32[]{:S(2)}, u32[]{:S(2)}) %collective-permute-start) | collective-permute-done | bytes 262176 | tf_op jit(solution)/shard_map/ppermute | solution.py:166
  10.3 2.0 %collective-permute-done.1.refs_1_ = bf16[128,1024]{1,0:T(8,128)(2,1)S(1)} collective-permute-done((bf16[128,1024]{1,0:T(8,128)(2,1)}, bf16[128,1024]{1,0:T(8,128)(2,1)S(1)}, u32[]{:S(2)}, u32[]{:S(2)}) %collective-permute-start.1) | collective-permute-done | bytes 262176 | tf_op jit(solution)/shard_map/ppermute | solution.py:166
  12.4 2.7 %collective-permute-done.2.refs_2_ = bf16[128,1024]{1,0:T(8,128)(2,1)S(1)} collective-permute-done((bf16[128,1024]{1,0:T(8,128)(2,1)}, bf16[128,1024]{1,0:T(8,128)(2,1)S(1)}, u32[]{:S(2)}, u32[]{:S(2)}) %collective-permute-start.2) | collective-permute-done | bytes 262176 | tf_op jit(solution)/shard_map/ppermute | solution.py:166
  15.1 3.9 %collective-permute-start.15 = (bf16[128,1024]{1,0:T(8,128)(2,1)}, bf16[128,1024]{1,0:T(8,128)(2,1)S(1)}, u32[]{:S(2)}, u32[]{:S(2)}) collective-permute-start(bf16[128,1024]{1,0:T(8,128)(2,1)} %teacher.1), channel_id=1, source_target_pairs={{0,24},{1,25},{2,26},{3,27},{4,28},{5,29},{6,30},{7,31},{24,8},{25... | collective-permute-start | bytes 786440 | tf_op jit(solution)/shard_map/ppermute | solution.py:166
  19.0 6.9 %collective-permute-done.4.refs_0_ = bf16[128,1024]{1,0:T(8,128)(2,1)S(1)} collective-permute-done((bf16[128,1024]{1,0:T(8,128)(2,1)}, bf16[128,1024]{1,0:T(8,128)(2,1)S(1)}, u32[]{:S(2)}, u32[]{:S(2)}) %collective-permute-start.4) | collective-permute-done | bytes 262176 | tf_op jit(solution)/shard_map/ppermute | solution.py:166
  25.8 1.6 %collective-permute-start.11 = (bf16[128,1024]{1,0:T(8,128)(2,1)S(1)}, bf16[128,1024]{1,0:T(8,128)(2,1)S(1)}, u32[]{:S(2)}, u32[]{:S(2)}) collective-permute-start(bf16[128,1024]{1,0:T(8,128)(2,1)S(1)} %collective-permute-done.refs_0_), channel_id=1, source_target_pairs={{0,4},{1,5},{2,6},{3,7},{4,0},{5,1},{6,2},{7,3},{8,12},{9,13},{10,... | collective-permute-start | bytes 786440 | tf_op jit(solution)/shard_map/ppermute | solution.py:166
  27.4 1.5 %collective-permute-start.13 = (bf16[128,1024]{1,0:T(8,128)(2,1)S(1)}, bf16[128,1024]{1,0:T(8,128)(2,1)S(1)}, u32[]{:S(2)}, u32[]{:S(2)}) collective-permute-start(bf16[128,1024]{1,0:T(8,128)(2,1)S(1)} %collective-permute-done.3.refs_3_), channel_id=1, source_target_pairs={{0,2},{1,3},{2,0},{3,1},{4,6},{5,7},{6,4},{7,5},{8,10},{9,11},{10,... | collective-permute-start | bytes 786440 | tf_op jit(solution)/shard_map/ppermute | solution.py:166
  28.9 1.4 %collective-permute-done.15.refs_0_ = bf16[128,1024]{1,0:T(8,128)(2,1)S(1)} collective-permute-done((bf16[128,1024]{1,0:T(8,128)(2,1)}, bf16[128,1024]{1,0:T(8,128)(2,1)S(1)}, u32[]{:S(2)}, u32[]{:S(2)}) %collective-permute-start.15) | collective-permute-done | bytes 262176 | tf_op jit(solution)/shard_map/ppermute | solution.py:166
  30.9 1.3 %collective-permute-done.11.refs_0_ = bf16[128,1024]{1,0:T(8,128)(2,1)S(1)} collective-permute-done((bf16[128,1024]{1,0:T(8,128)(2,1)S(1)}, bf16[128,1024]{1,0:T(8,128)(2,1)S(1)}, u32[]{:S(2)}, u32[]{:S(2)}) %collective-permute-start.11) | collective-permute-done | bytes 262176 | tf_op jit(solution)/shard_map/ppermute | solution.py:166
  32.2 1.6 %collective-permute-done.13.refs_2_ = bf16[128,1024]{1,0:T(8,128)(2,1)S(1)} collective-permute-done((bf16[128,1024]{1,0:T(8,128)(2,1)S(1)}, bf16[128,1024]{1,0:T(8,128)(2,1)S(1)}, u32[]{:S(2)}, u32[]{:S(2)}) %collective-permute-start.13) | collective-permute-done | bytes 262176 | tf_op jit(solution)/shard_map/ppermute | solution.py:166
  33.8 1.0 %copy-done = bf16[128,1024]{1,0:T(8,128)(2,1)S(1)} copy-done((bf16[128,1024]{1,0:T(8,128)(2,1)S(1)}, bf16[128,1024]{1,0:T(8,128)(2,1)}, u32[]{:S(2)}) %copy-start) | copy-done | bytes 262168
  34.8 0.9 %copy-done.1 = bf16[128,1024]{1,0:T(8,128)(2,1)S(1)} copy-done((bf16[128,1024]{1,0:T(8,128)(2,1)S(1)}, bf16[128,1024]{1,0:T(8,128)(2,1)}, u32[]{:S(2)}) %copy-start.1) | copy-done | bytes 262168
  36.9 1.6 %collective-permute-start.20 = (bf16[128,1024]{1,0:T(8,128)(2,1)S(1)}, bf16[128,1024]{1,0:T(8,128)(2,1)S(1)}, u32[]{:S(2)}, u32[]{:S(2)}) collective-permute-start(bf16[128,1024]{1,0:T(8,128)(2,1)S(1)} %get-tuple-element.31.once_s.refs_3_), channel_id=1, source_target_pairs={{0,2},{1,3},{2,0},{3,1},{4,6},{5,7},{6,4},{7,5},{8,10},{9,11},{10,... | collective-permute-start | bytes 786440 | tf_op jit(solution)/shard_map/ppermute | solution.py:166
  39.0 2.0 %collective-permute-start.27 = (bf16[128,1024]{1,0:T(8,128)(2,1)S(1)}, bf16[128,1024]{1,0:T(8,128)(2,1)S(1)}, u32[]{:S(2)}, u32[]{:S(2)}) collective-permute-start(bf16[128,1024]{1,0:T(8,128)(2,1)S(1)} %copy-done.2), channel_id=1, source_target_pairs={{0,8},{1,9},{2,10},{3,11},{4,12},{5,13},{6,14},{7,15},{24,16},{25,... | collective-permute-start | bytes 786440 | tf_op jit(solution)/shard_map/ppermute | solution.py:166
  41.0 0.7 %shard_map.31 = (bf16[1024,1024]{1,0:T(8,128)(2,1)S(1)}, bf16[1024,1024]{1,0:T(8,128)(2,1)S(1)}, f32[1024,128]{1,0:T(8,128)S(1)}) custom-call(bf16[1024,1024]{1,0:T(8,128)(2,1)S(1)} %get-tuple-element.28.block_s, bf16[1024,1024]{1,0:T(8,128)(2,1)S(1)} %get-tuple-element.29.block_t, ...), custom_call_target="tpu_custom_call", output_to_operand_aliasing={{0}: (0, {}), {1}: (1, {}), {2}: (2, {})} | custom-call | flops 100663296 | bytes 11272192 | tf_op jit(solution)/shard_map/pallas_call | solution.py:39
  42.1 1.3 %shard_map.34 = (bf16[512,128]{1,0:T(8,128)(2,1)S(1)}, bf16[512,128]{1,0:T(8,128)(2,1)S(1)}, bf16[128,1024]{1,0:T(8,128)(2,1)S(1)}) custom-call(bf16[1024,1024]{1,0:T(8,128)(2,1)S(1)} %get-tuple-element.35.block_s, bf16[1024,1024]{1,0:T(8,128)(2,1)S(1)} %get-tuple-element.36.block_t, f32[1024,128]{1,0:T(8,128)S(1)} %get-tuple-element.37.product, ...), custom_call_target="tpu_custom_call" | custom-call | flops 536870912 | bytes 5505024 | tf_op jit(solution)/shard_map/pallas_call | solution.py:39
  43.4 0.6 collective-permute-start.16
  44.0 1.7 %collective-permute-done.20.refs_5_ = bf16[128,1024]{1,0:T(8,128)(2,1)S(1)} collective-permute-done((bf16[128,1024]{1,0:T(8,128)(2,1)S(1)}, bf16[128,1024]{1,0:T(8,128)(2,1)S(1)}, u32[]{:S(2)}, u32[]{:S(2)}) %collective-permute-start.20) | collective-permute-done | bytes 262176 | tf_op jit(solution)/shard_map/ppermute | solution.py:166
  45.7 1.2 %collective-permute-done.22.refs_7_ = bf16[128,1024]{1,0:T(8,128)(2,1)S(1)} collective-permute-done((bf16[128,1024]{1,0:T(8,128)(2,1)S(1)}, bf16[128,1024]{1,0:T(8,128)(2,1)S(1)}, u32[]{:S(2)}, u32[]{:S(2)}) %collective-permute-start.22) | collective-permute-done | bytes 262176 | tf_op jit(solution)/shard_map/ppermute | solution.py:166
  46.9 1.5 %collective-permute-done.27.refs_1_ = bf16[128,1024]{1,0:T(8,128)(2,1)S(1)} collective-permute-done((bf16[128,1024]{1,0:T(8,128)(2,1)S(1)}, bf16[128,1024]{1,0:T(8,128)(2,1)S(1)}, u32[]{:S(2)}, u32[]{:S(2)}) %collective-permute-start.27) | collective-permute-done | bytes 262176 | tf_op jit(solution)/shard_map/ppermute | solution.py:166
  48.4 1.7 %collective-permute-start.24 = (bf16[128,1024]{1,0:T(8,128)(2,1)S(1)}, bf16[128,1024]{1,0:T(8,128)(2,1)S(1)}, u32[]{:S(2)}, u32[]{:S(2)}) collective-permute-start(bf16[128,1024]{1,0:T(8,128)(2,1)S(1)} %get-tuple-element.43), channel_id=1, source_target_pairs={{0,16},{1,17},{2,18},{3,19},{4,20},{5,21},{6,22},{7,23},{24,0},{25... | collective-permute-start | bytes 786440 | tf_op jit(solution)/shard_map/ppermute | solution.py:166
  50.1 1.8 %shard_map.37 = bf16[128,1024]{1,0:T(8,128)(2,1)S(1)} custom-call(bf16[1024,1024]{1,0:T(8,128)(2,1)S(1)} %get-tuple-element.35.block_s, bf16[1024,1024]{1,0:T(8,128)(2,1)S(1)} %get-tuple-element.36.block_t, bf16[128,1024]{1,0:T(8,128)(2,1)S(1)} %collective-permute-done.26.refs_0_, bf16[128,1024]{1,0:T(8,128)(2,1)S(1)} %collective-permute-done.27.refs_1_), custom_call_target="tpu_custom_call" | custom-call | flops 805306368 | bytes 4980736 | tf_op jit(solution)/shard_map/pallas_call | solution.py:39
  51.9 0.6 collective-permute-start.28
  52.8 1.6 %collective-permute-start.25 = (bf16[128,1024]{1,0:T(8,128)(2,1)S(1)}, bf16[128,1024]{1,0:T(8,128)(2,1)S(1)}, u32[]{:S(2)}, u32[]{:S(2)}) collective-permute-start(bf16[128,1024]{1,0:T(8,128)(2,1)S(1)} %get-tuple-element.44), channel_id=1, source_target_pairs={{0,6},{1,7},{2,4},{3,5},{4,2},{5,3},{6,0},{7,1},{8,14},{9,15},{10,... | collective-permute-start | bytes 786440 | tf_op jit(solution)/shard_map/ppermute | solution.py:166
  54.3 1.5 %collective-permute-start.18 = (bf16[128,256]{1,0:T(8,128)(2,1)S(1)}, bf16[128,256]{1,0:T(8,128)(2,1)S(1)}, u32[]{:S(2)}, u32[]{:S(2)}) collective-permute-start(bf16[128,256]{1,0:T(8,128)(2,1)S(1)} %get-tuple-element.41), channel_id=1, source_target_pairs={{0,2},{1,3},{2,0},{3,1},{4,6},{5,7},{6,4},{7,5},{8,10},{9,11},{10,... | collective-permute-start | bytes 196616 | tf_op jit(solution)/shard_map/ppermute | solution.py:166
  56.3 1.6 %shard_map.33.before = f32[128,1024]{1,0:T(8,128)S(1)} custom-call(bf16[128,1024]{1,0:T(8,128)(2,1)S(1)} %get-tuple-element.25.own_s, bf16[128,1024]{1,0:T(8,128)(2,1)S(1)} %get-tuple-element.27.own_t, bf16[1024,1024]{1,0:T(8,128)(2,1)S(1)} %get-tuple-element.35.block_s, bf16[1024,1024]{1,0:T(8,128)(2,1)S(1)} %get-tuple-element.36.block_t), custom_call_target="tpu_custom_call" | custom-call | flops 805306368 | bytes 5242880 | tf_op jit(solution)/shard_map/pallas_call | solution.py:39
  57.9 4.2 %collective-permute-done.18.refs_1_ = bf16[128,256]{1,0:T(8,128)(2,1)S(1)} collective-permute-done((bf16[128,256]{1,0:T(8,128)(2,1)S(1)}, bf16[128,256]{1,0:T(8,128)(2,1)S(1)}, u32[]{:S(2)}, u32[]{:S(2)}) %collective-permute-start.18) | collective-permute-done | bytes 65568 | tf_op jit(solution)/shard_map/ppermute | solution.py:166
  62.1 0.9 %collective-permute-done.19.refs_2_ = bf16[128,256]{1,0:T(8,128)(2,1)S(1)} collective-permute-done((bf16[128,256]{1,0:T(8,128)(2,1)S(1)}, bf16[128,256]{1,0:T(8,128)(2,1)S(1)}, u32[]{:S(2)}, u32[]{:S(2)}) %collective-permute-start.19) | collective-permute-done | bytes 65568 | tf_op jit(solution)/shard_map/ppermute | solution.py:166
  63.7 1.1 %shard_map.38 = f32[128,1024]{1,0:T(8,128)} custom-call(bf16[128,1024]{1,0:T(8,128)(2,1)S(1)} %get-tuple-element.25.own_s, f32[128,128]{1,0:T(8,128)S(1)} %get-tuple-element.26.scale, f32[128,1024]{1,0:T(8,128)S(1)} %shard_map.36.refs_0_, bf16[128,1024]{1,0:T(8,128)(2,1)S(1)} %collective-permute-done.24.refs_1_, ...), custom_call_target="tpu_custom_call" | custom-call | bytes 2162688 | tf_op jit(solution)/shard_map/pallas_call | solution.py:39
  (43 shorter events, 4.7 us)
Async XLA Ops:
  0.0 10.3 %collective-permute-start = (bf16[128,1024]{1,0:T(8,128)(2,1)}, bf16[128,1024]{1,0:T(8,128)(2,1)S(1)}, u32[]{:S(2)}, u32[]{:S(2)}) collective-permute-start(bf16[128,1024]{1,0:T(8,128)(2,1)} %student.1), channel_id=1, source_target_pairs={{0,2},{1,3},{2,0},{3,1},{4,6},{5,7},{6,4},{7,5},{8,10},{9,11},{10,... | collective-permute-start | bytes 786440 | tf_op jit(solution)/shard_map/ppermute | solution.py:166
  3.0 9.4 %collective-permute-start.1 = (bf16[128,1024]{1,0:T(8,128)(2,1)}, bf16[128,1024]{1,0:T(8,128)(2,1)S(1)}, u32[]{:S(2)}, u32[]{:S(2)}) collective-permute-start(bf16[128,1024]{1,0:T(8,128)(2,1)} %student.1), channel_id=1, source_target_pairs={{0,4},{1,5},{2,6},{3,7},{4,0},{5,1},{6,2},{7,3},{8,12},{9,13},{10,... | collective-permute-start | bytes 786440 | tf_op jit(solution)/shard_map/ppermute | solution.py:166
  4.5 10.6 %collective-permute-start.2 = (bf16[128,1024]{1,0:T(8,128)(2,1)}, bf16[128,1024]{1,0:T(8,128)(2,1)S(1)}, u32[]{:S(2)}, u32[]{:S(2)}) collective-permute-start(bf16[128,1024]{1,0:T(8,128)(2,1)} %teacher.1), channel_id=1, source_target_pairs={{0,2},{1,3},{2,0},{3,1},{4,6},{5,7},{6,4},{7,5},{8,10},{9,11},{10,... | collective-permute-start | bytes 786440 | tf_op jit(solution)/shard_map/ppermute | solution.py:166
  5.0 13.9 %collective-permute-start.3 = (bf16[128,1024]{1,0:T(8,128)(2,1)}, bf16[128,1024]{1,0:T(8,128)(2,1)S(1)}, u32[]{:S(2)}, u32[]{:S(2)}) collective-permute-start(bf16[128,1024]{1,0:T(8,128)(2,1)} %teacher.1), channel_id=1, source_target_pairs={{0,4},{1,5},{2,6},{3,7},{4,0},{5,1},{6,2},{7,3},{8,12},{9,13},{10,... | collective-permute-start | bytes 786440 | tf_op jit(solution)/shard_map/ppermute | solution.py:166
  5.0 20.8 %collective-permute-start.4 = (bf16[128,1024]{1,0:T(8,128)(2,1)}, bf16[128,1024]{1,0:T(8,128)(2,1)S(1)}, u32[]{:S(2)}, u32[]{:S(2)}) collective-permute-start(bf16[128,1024]{1,0:T(8,128)(2,1)} %student.1), channel_id=1, source_target_pairs={{0,24},{1,25},{2,26},{3,27},{4,28},{5,29},{6,30},{7,31},{24,8},{25... | collective-permute-start | bytes 786440 | tf_op jit(solution)/shard_map/ppermute | solution.py:166
  10.3 17.1 %collective-permute-start.5 = (bf16[128,1024]{1,0:T(8,128)(2,1)}, bf16[128,1024]{1,0:T(8,128)(2,1)S(1)}, u32[]{:S(2)}, u32[]{:S(2)}) collective-permute-start(bf16[128,1024]{1,0:T(8,128)(2,1)} %student.1), channel_id=1, source_target_pairs={{0,1},{1,0},{2,3},{3,2},{4,5},{5,4},{6,7},{7,6},{8,9},{9,8},{10,11... | collective-permute-start | bytes 786440 | tf_op jit(solution)/shard_map/ppermute | solution.py:166
  12.4 16.6 %collective-permute-start.8 = (bf16[128,1024]{1,0:T(8,128)(2,1)}, bf16[128,1024]{1,0:T(8,128)(2,1)S(1)}, u32[]{:S(2)}, u32[]{:S(2)}) collective-permute-start(bf16[128,1024]{1,0:T(8,128)(2,1)} %teacher.1), channel_id=1, source_target_pairs={{0,1},{1,0},{2,3},{3,2},{4,5},{5,4},{6,7},{7,6},{8,9},{9,8},{10,11... | collective-permute-start | bytes 786440 | tf_op jit(solution)/shard_map/ppermute | solution.py:166
  15.1 15.3 %collective-permute-start.15 = (bf16[128,1024]{1,0:T(8,128)(2,1)}, bf16[128,1024]{1,0:T(8,128)(2,1)S(1)}, u32[]{:S(2)}, u32[]{:S(2)}) collective-permute-start(bf16[128,1024]{1,0:T(8,128)(2,1)} %teacher.1), channel_id=1, source_target_pairs={{0,24},{1,25},{2,26},{3,27},{4,28},{5,29},{6,30},{7,31},{24,8},{25... | collective-permute-start | bytes 786440 | tf_op jit(solution)/shard_map/ppermute | solution.py:166
  19.0 11.4 %collective-permute-start.6 = (bf16[128,1024]{1,0:T(8,128)(2,1)S(1)}, bf16[128,1024]{1,0:T(8,128)(2,1)S(1)}, u32[]{:S(2)}, u32[]{:S(2)}) collective-permute-start(bf16[128,1024]{1,0:T(8,128)(2,1)S(1)} %collective-permute-done.refs_0_), channel_id=1, source_target_pairs={{0,1},{1,0},{2,3},{3,2},{4,5},{5,4},{6,7},{7,6},{8,9},{9,8},{10,11... | collective-permute-start | bytes 786440 | tf_op jit(solution)/shard_map/ppermute | solution.py:166
  25.8 6.4 %collective-permute-start.11 = (bf16[128,1024]{1,0:T(8,128)(2,1)S(1)}, bf16[128,1024]{1,0:T(8,128)(2,1)S(1)}, u32[]{:S(2)}, u32[]{:S(2)}) collective-permute-start(bf16[128,1024]{1,0:T(8,128)(2,1)S(1)} %collective-permute-done.refs_0_), channel_id=1, source_target_pairs={{0,4},{1,5},{2,6},{3,7},{4,0},{5,1},{6,2},{7,3},{8,12},{9,13},{10,... | collective-permute-start | bytes 786440 | tf_op jit(solution)/shard_map/ppermute | solution.py:166
  27.4 6.4 %collective-permute-start.13 = (bf16[128,1024]{1,0:T(8,128)(2,1)S(1)}, bf16[128,1024]{1,0:T(8,128)(2,1)S(1)}, u32[]{:S(2)}, u32[]{:S(2)}) collective-permute-start(bf16[128,1024]{1,0:T(8,128)(2,1)S(1)} %collective-permute-done.3.refs_3_), channel_id=1, source_target_pairs={{0,2},{1,3},{2,0},{3,1},{4,6},{5,7},{6,4},{7,5},{8,10},{9,11},{10,... | collective-permute-start | bytes 786440 | tf_op jit(solution)/shard_map/ppermute | solution.py:166
  28.9 4.9 %collective-permute-start.7 = (bf16[128,1024]{1,0:T(8,128)(2,1)S(1)}, bf16[128,1024]{1,0:T(8,128)(2,1)S(1)}, u32[]{:S(2)}, u32[]{:S(2)}) collective-permute-start(bf16[128,1024]{1,0:T(8,128)(2,1)S(1)} %collective-permute-done.1.refs_1_), channel_id=1, source_target_pairs={{0,1},{1,0},{2,3},{3,2},{4,5},{5,4},{6,7},{7,6},{8,9},{9,8},{10,11... | collective-permute-start | bytes 786440 | tf_op jit(solution)/shard_map/ppermute | solution.py:166
  30.4 6.5 %collective-permute-start.9 = (bf16[128,1024]{1,0:T(8,128)(2,1)S(1)}, bf16[128,1024]{1,0:T(8,128)(2,1)S(1)}, u32[]{:S(2)}, u32[]{:S(2)}) collective-permute-start(bf16[128,1024]{1,0:T(8,128)(2,1)S(1)} %collective-permute-done.2.refs_2_), channel_id=1, source_target_pairs={{0,1},{1,0},{2,3},{3,2},{4,5},{5,4},{6,7},{7,6},{8,9},{9,8},{10,11... | collective-permute-start | bytes 786440 | tf_op jit(solution)/shard_map/ppermute | solution.py:166
  30.4 8.1 %collective-permute-start.10 = (bf16[128,1024]{1,0:T(8,128)(2,1)S(1)}, bf16[128,1024]{1,0:T(8,128)(2,1)S(1)}, u32[]{:S(2)}, u32[]{:S(2)}) collective-permute-start(bf16[128,1024]{1,0:T(8,128)(2,1)S(1)} %collective-permute-done.3.refs_3_), channel_id=1, source_target_pairs={{0,1},{1,0},{2,3},{3,2},{4,5},{5,4},{6,7},{7,6},{8,9},{9,8},{10,11... | collective-permute-start | bytes 786440 | tf_op jit(solution)/shard_map/ppermute | solution.py:166
  32.2 6.8 %collective-permute-start.12 = (bf16[128,1024]{1,0:T(8,128)(2,1)S(1)}, bf16[128,1024]{1,0:T(8,128)(2,1)S(1)}, u32[]{:S(2)}, u32[]{:S(2)}) collective-permute-start(bf16[128,1024]{1,0:T(8,128)(2,1)S(1)} %collective-permute-done.11.refs_0_), channel_id=1, source_target_pairs={{0,1},{1,0},{2,3},{3,2},{4,5},{5,4},{6,7},{7,6},{8,9},{9,8},{10,11... | collective-permute-start | bytes 786440 | tf_op jit(solution)/shard_map/ppermute | solution.py:166
  33.8 7.2 %collective-permute-start.14 = (bf16[128,1024]{1,0:T(8,128)(2,1)S(1)}, bf16[128,1024]{1,0:T(8,128)(2,1)S(1)}, u32[]{:S(2)}, u32[]{:S(2)}) collective-permute-start(bf16[128,1024]{1,0:T(8,128)(2,1)S(1)} %collective-permute-done.13.refs_2_), channel_id=1, source_target_pairs={{0,1},{1,0},{2,3},{3,2},{4,5},{5,4},{6,7},{7,6},{8,9},{9,8},{10,11... | collective-permute-start | bytes 786440 | tf_op jit(solution)/shard_map/ppermute | solution.py:166
  33.8 9.6 %collective-permute-start.26 = (bf16[128,1024]{1,0:T(8,128)(2,1)}, bf16[128,1024]{1,0:T(8,128)(2,1)S(1)}, u32[]{:S(2)}, u32[]{:S(2)}) collective-permute-start(bf16[128,1024]{1,0:T(8,128)(2,1)} %student.1), channel_id=1, source_target_pairs={{0,8},{1,9},{2,10},{3,11},{4,12},{5,13},{6,14},{7,15},{24,16},{25,... | collective-permute-start | bytes 786440 | tf_op jit(solution)/shard_map/ppermute | solution.py:166
  33.8 1.0 %copy-start = (bf16[128,1024]{1,0:T(8,128)(2,1)S(1)}, bf16[128,1024]{1,0:T(8,128)(2,1)}, u32[]{:S(2)}) copy-start(bf16[128,1024]{1,0:T(8,128)(2,1)} %student.1) | copy-start | bytes 786436
  34.8 0.9 %copy-start.1 = (bf16[128,1024]{1,0:T(8,128)(2,1)S(1)}, bf16[128,1024]{1,0:T(8,128)(2,1)}, u32[]{:S(2)}) copy-start(bf16[128,1024]{1,0:T(8,128)(2,1)} %teacher.1) | copy-start | bytes 786436
  36.0 3.0 %copy-start.2 = (bf16[128,1024]{1,0:T(8,128)(2,1)S(1)}, bf16[128,1024]{1,0:T(8,128)(2,1)}, u32[]{:S(2)}) copy-start(bf16[128,1024]{1,0:T(8,128)(2,1)} %teacher.1) | copy-start | bytes 786436
  36.9 8.8 %collective-permute-start.20 = (bf16[128,1024]{1,0:T(8,128)(2,1)S(1)}, bf16[128,1024]{1,0:T(8,128)(2,1)S(1)}, u32[]{:S(2)}, u32[]{:S(2)}) collective-permute-start(bf16[128,1024]{1,0:T(8,128)(2,1)S(1)} %get-tuple-element.31.once_s.refs_3_), channel_id=1, source_target_pairs={{0,2},{1,3},{2,0},{3,1},{4,6},{5,7},{6,4},{7,5},{8,10},{9,11},{10,... | collective-permute-start | bytes 786440 | tf_op jit(solution)/shard_map/ppermute | solution.py:166
  38.4 8.4 %collective-permute-start.22 = (bf16[128,1024]{1,0:T(8,128)(2,1)S(1)}, bf16[128,1024]{1,0:T(8,128)(2,1)S(1)}, u32[]{:S(2)}, u32[]{:S(2)}) collective-permute-start(bf16[128,1024]{1,0:T(8,128)(2,1)S(1)} %get-tuple-element.31.once_s.refs_3_), channel_id=1, source_target_pairs={{0,4},{1,5},{2,6},{3,7},{4,0},{5,1},{6,2},{7,3},{8,12},{9,13},{10,... | collective-permute-start | bytes 786440 | tf_op jit(solution)/shard_map/ppermute | solution.py:166
  39.0 9.4 %collective-permute-start.27 = (bf16[128,1024]{1,0:T(8,128)(2,1)S(1)}, bf16[128,1024]{1,0:T(8,128)(2,1)S(1)}, u32[]{:S(2)}, u32[]{:S(2)}) collective-permute-start(bf16[128,1024]{1,0:T(8,128)(2,1)S(1)} %copy-done.2), channel_id=1, source_target_pairs={{0,8},{1,9},{2,10},{3,11},{4,12},{5,13},{6,14},{7,15},{24,16},{25,... | collective-permute-start | bytes 786440 | tf_op jit(solution)/shard_map/ppermute | solution.py:166
  41.0 10.9 %collective-permute-start.17 = (bf16[128,1024]{1,0:T(8,128)(2,1)S(1)}, bf16[128,1024]{1,0:T(8,128)(2,1)S(1)}, u32[]{:S(2)}, u32[]{:S(2)}) collective-permute-start(bf16[128,1024]{1,0:T(8,128)(2,1)S(1)} %get-tuple-element.31.once_s.refs_3_), channel_id=1, source_target_pairs={{0,1},{1,0},{2,3},{3,2},{4,5},{5,4},{6,7},{7,6},{8,9},{9,8},{10,11... | collective-permute-start | bytes 786440 | tf_op jit(solution)/shard_map/ppermute | solution.py:166
  43.4 9.0 %collective-permute-start.16 = (bf16[512,128]{1,0:T(8,128)(2,1)S(1)}, bf16[512,128]{1,0:T(8,128)(2,1)S(1)}, u32[]{:S(2)}, u32[]{:S(2)}) collective-permute-start(bf16[512,128]{1,0:T(8,128)(2,1)S(1)} %get-tuple-element.39), channel_id=1, source_target_pairs={{0,1},{1,0},{2,3},{3,2},{4,5},{5,4},{6,7},{7,6},{8,9},{9,8},{10,11... | collective-permute-start | bytes 393224 | tf_op jit(solution)/shard_map/ppermute | solution.py:166
  45.7 8.7 %collective-permute-start.21 = (bf16[128,1024]{1,0:T(8,128)(2,1)S(1)}, bf16[128,1024]{1,0:T(8,128)(2,1)S(1)}, u32[]{:S(2)}, u32[]{:S(2)}) collective-permute-start(bf16[128,1024]{1,0:T(8,128)(2,1)S(1)} %collective-permute-done.20.refs_5_), channel_id=1, source_target_pairs={{0,1},{1,0},{2,3},{3,2},{4,5},{5,4},{6,7},{7,6},{8,9},{9,8},{10,11... | collective-permute-start | bytes 786440 | tf_op jit(solution)/shard_map/ppermute | solution.py:166
  46.9 8.9 %collective-permute-start.23 = (bf16[128,1024]{1,0:T(8,128)(2,1)S(1)}, bf16[128,1024]{1,0:T(8,128)(2,1)S(1)}, u32[]{:S(2)}, u32[]{:S(2)}) collective-permute-start(bf16[128,1024]{1,0:T(8,128)(2,1)S(1)} %collective-permute-done.22.refs_7_), channel_id=1, source_target_pairs={{0,1},{1,0},{2,3},{3,2},{4,5},{5,4},{6,7},{7,6},{8,9},{9,8},{10,11... | collective-permute-start | bytes 786440 | tf_op jit(solution)/shard_map/ppermute | solution.py:166
  48.4 15.1 %collective-permute-start.24 = (bf16[128,1024]{1,0:T(8,128)(2,1)S(1)}, bf16[128,1024]{1,0:T(8,128)(2,1)S(1)}, u32[]{:S(2)}, u32[]{:S(2)}) collective-permute-start(bf16[128,1024]{1,0:T(8,128)(2,1)S(1)} %get-tuple-element.43), channel_id=1, source_target_pairs={{0,16},{1,17},{2,18},{3,19},{4,20},{5,21},{6,22},{7,23},{24,0},{25... | collective-permute-start | bytes 786440 | tf_op jit(solution)/shard_map/ppermute | solution.py:166
  51.9 11.8 %collective-permute-start.28 = (bf16[128,1024]{1,0:T(8,128)(2,1)S(1)}, bf16[128,1024]{1,0:T(8,128)(2,1)S(1)}, u32[]{:S(2)}, u32[]{:S(2)}) collective-permute-start(bf16[128,1024]{1,0:T(8,128)(2,1)S(1)} %shard_map.37), channel_id=1, source_target_pairs={{0,8},{1,9},{2,10},{3,11},{4,12},{5,13},{6,14},{7,15},{24,16},{25,... | collective-permute-start | bytes 786440 | tf_op jit(solution)/shard_map/ppermute | solution.py:166
  52.8 11.0 %collective-permute-start.25 = (bf16[128,1024]{1,0:T(8,128)(2,1)S(1)}, bf16[128,1024]{1,0:T(8,128)(2,1)S(1)}, u32[]{:S(2)}, u32[]{:S(2)}) collective-permute-start(bf16[128,1024]{1,0:T(8,128)(2,1)S(1)} %get-tuple-element.44), channel_id=1, source_target_pairs={{0,6},{1,7},{2,4},{3,5},{4,2},{5,3},{6,0},{7,1},{8,14},{9,15},{10,... | collective-permute-start | bytes 786440 | tf_op jit(solution)/shard_map/ppermute | solution.py:166
  54.3 7.8 %collective-permute-start.18 = (bf16[128,256]{1,0:T(8,128)(2,1)S(1)}, bf16[128,256]{1,0:T(8,128)(2,1)S(1)}, u32[]{:S(2)}, u32[]{:S(2)}) collective-permute-start(bf16[128,256]{1,0:T(8,128)(2,1)S(1)} %get-tuple-element.41), channel_id=1, source_target_pairs={{0,2},{1,3},{2,0},{3,1},{4,6},{5,7},{6,4},{7,5},{8,10},{9,11},{10,... | collective-permute-start | bytes 196616 | tf_op jit(solution)/shard_map/ppermute | solution.py:166
  55.8 7.2 %collective-permute-start.19 = (bf16[128,256]{1,0:T(8,128)(2,1)S(1)}, bf16[128,256]{1,0:T(8,128)(2,1)S(1)}, u32[]{:S(2)}, u32[]{:S(2)}) collective-permute-start(bf16[128,256]{1,0:T(8,128)(2,1)S(1)} %get-tuple-element.42), channel_id=1, source_target_pairs={{0,4},{1,5},{2,6},{3,7},{4,0},{5,1},{6,2},{7,3},{8,12},{9,13},{10,... | collective-permute-start | bytes 196616 | tf_op jit(solution)/shard_map/ppermute | solution.py:166
